TPU v7x, 256 devices: a whole 4x4x8 slice. The times are simulated.
256 devices in a mesh: box: 32 (over y, z_lo, x), row: 8 (over z_hi, core).
Axes of the slice: x: 4, y: 4, z: 8 (z_hi: 4, z_lo: 2; z = z_hi * 2 + z_lo), core: 2. Of those that a mesh axis runs over, the one named last changes fastest.
Arguments:
- dtn_map: float32 [64, 4, 128, 512], P('box', None, 'row'), as said below
- boundary_data: bfloat16 [64, 3, 128, 768], P('box'), may hold values from -6 to 6
- solution_op: bfloat16 [64, 16384, 512], P('box', 'row'), may hold values from -0.25 to 0.25
Outputs:
- parent_map: float32 [64, 3, 128, 768], P('box', None, 'row')
- interior_field: bfloat16 [64, 16384, 768], P('box', 'row')
Inputs may be any that keep to these rules, and one draw needn't show every extreme that they name: `dtn_map`: in the 128 x 128 block that couples each side with itself, every map is symmetric and its diagonal exceeds the sum of the magnitudes of the rest of the block's row by 0.1 or more.
All inputs are finite; a program needn't handle non-finite values.
Results may differ from a plain program's by a relative error of at most 0.0027.
Values may be sent and summed in bfloat16 or wider, within the bound.
No kernel may reach another device: no remote copies, remote signals or barrier semaphores. Data moves between devices by JAX's collectives and lax.ppermute only.
A program may use at most 64 MiB of HBM per device.

v0:
```python
import jax
import jax.numpy as jnp
from jax import lax
from jax.sharding import PartitionSpec as P


def from_partner(value, axis, stride):
    mask = 2**stride
    pairs = [(source, source ^ mask) for source in range(lax.axis_size(axis))]
    return lax.ppermute(value, axis, pairs)


def invert_factor(factor):
    identity = jnp.broadcast_to(jnp.eye(factor.shape[1], dtype=jnp.float32), factor.shape)
    return lax.linalg.triangular_solve(factor, identity, left_side=True, lower=True)


def solve_shared(inverse_factor, right_side):
    highest = lax.Precision.HIGHEST
    lower_part = jnp.einsum("bij,bjq->biq", inverse_factor, right_side, precision=highest)
    return jnp.einsum("bji,bjq->biq", inverse_factor, lower_part, precision=highest)


def per_device(dtn_map, boundary_data, solution_op):
    box_count = dtn_map.shape[0]
    edge_size = boundary_data.shape[2]
    outer_size = 3 * edge_size
    loads_count = boundary_data.shape[3]
    highest = lax.Precision.HIGHEST
    is_alpha = lax.axis_index("box") % 2 == 0
    own_local = dtn_map[:, 3]
    own_edge = lax.all_gather(own_local, "row", axis=1, tiled=True)
    other_edge = from_partner(own_edge, "box", 0)
    alpha_edge = jnp.where(is_alpha, own_edge, other_edge)
    beta_edge = jnp.where(is_alpha, other_edge, own_edge)
    shared_block = alpha_edge[:, :, outer_size:] + beta_edge[:, :, outer_size:]
    factor = jnp.linalg.cholesky(shared_block)
    inverse_factor = invert_factor(factor)
    coupling = jnp.concatenate(
        [alpha_edge[:, :, :outer_size], beta_edge[:, :, :outer_size]], axis=2
    )
    transfer = -solve_shared(inverse_factor, coupling)
    local_rows = dtn_map[:, :3].reshape(box_count, -1, 4 * edge_size)
    outer_block = local_rows[:, :, :outer_size]
    blank_block = jnp.zeros(outer_block.shape, jnp.float32)
    placed = jnp.where(
        is_alpha,
        jnp.concatenate([outer_block, blank_block], axis=2),
        jnp.concatenate([blank_block, outer_block], axis=2),
    )
    correction = jnp.einsum(
        "brs,bsc->brc", local_rows[:, :, outer_size:], transfer, precision=highest
    )
    parent_map = (placed + correction).reshape(box_count, 3, -1, 6 * edge_size)
    own_data = boundary_data.reshape(box_count, outer_size, loads_count)
    own_float = own_data.astype(jnp.float32)
    own_terms = jnp.einsum(
        "bso,boq->bsq", own_edge[:, :, :outer_size], own_float, precision=highest
    )
    other_terms = from_partner(own_terms, "box", 0)
    summed = own_terms + other_terms
    edge_values = (-solve_shared(inverse_factor, summed)).astype(jnp.bfloat16)
    outer_part = jnp.einsum(
        "bro,boq->brq", solution_op[:, :, :outer_size], own_data, preferred_element_type=jnp.float32
    )
    edge_part = jnp.einsum(
        "brs,bsq->brq",
        solution_op[:, :, outer_size:],
        edge_values,
        preferred_element_type=jnp.float32,
    )
    interior_field = (outer_part + edge_part).astype(jnp.bfloat16)
    return (parent_map, interior_field)


def solution(mesh):
    in_specs = (P("box", None, "row", None), P("box", None, None, None), P("box", "row", None))
    out_specs = (P("box", None, "row", None), P("box", "row", None))
    return jax.shard_map(
        per_device, mesh=mesh, in_specs=in_specs, out_specs=out_specs, check_vma=False
    )
```

profile of v0, /device:TPU:1, one launch (start us, length us, event | category | flops | bytes accessed | tf_op | source)
XLA Modules:
  0.0 99.2 jit_solution(1274330110545535993)
XLA Ops:
  0.6 0.0 copy-start
  0.6 0.0 copy-start.2
  0.7 1.0 slice.45
  1.6 0.1 copy.33
  1.7 20.0 %all-gather = f32[2,1,128,512]{3,0,1,2:T(2,128)S(1)} all-gather(f32[2,1,16,512]{3,0,1,2:T(2,128)S(1)} %copy.33), channel_id=2, replica_groups=mesh['box'=32,'row'=8] {'row'}, dimensions={2}, use_global_device_ids=true | all-gather | bytes 589824 | tf_op jit(solution)/shard_map/all_gather | solution.py:32
  21.6 0.2 copy.17
  21.9 1.3 %collective-permute-start = (f32[2,128,512]{1,2,0:T(8,128)S(1)}, f32[2,128,512]{1,2,0:T(8,128)}, u32[]{:S(2)}, u32[]{:S(2)}) collective-permute-start(f32[2,128,512]{1,2,0:T(8,128)S(1)} %bitcast.35), channel_id=1, source_target_pairs={{0,8},{8,0},{16,24},{24,16},{32,40},{40,32},{48,56},{56,48},{64,72... | collective-permute-start | bytes 1572872 | tf_op jit(solution)/shard_map/ppermute | solution.py:10
  23.2 0.0 copy-done
  23.2 0.8 fusion.12
  24.0 0.3 collective-permute-start.1
  24.4 0.6 iota_compare_fusion
  25.0 0.6 fusion.19
  25.6 0.0 copy-done.2
  25.6 0.0 copy-start.1
  25.7 0.7 slice.54
  26.3 9.9 %fusion.1 = f32[2,2048,768]{2,1,0:T(8,128)} fusion(bf16[2,384,768]{2,1,0:T(8,128)(2,1)S(1)} %bitcast.33, bf16[2,2048,512]{2,1,0:T(8,128)(2,1)} %param.5), kind=kOutput, calls=%fused_computation.2 | convolution fusion | flops 2415919104 | bytes 16908288 | tf_op jit(solution)/shard_map/bro,boq->brq/dot_general | solution.py:63
  36.2 0.0 collective-permute-done
  36.2 1.1 %broadcast_select_fusion.1 = (f32[2,128,512]{1,2,0:T(8,128)S(1)}, f32[2,128,512]{1,2,0:T(8,128)S(1)}) fusion(f32[2,128,512]{1,2,0:T(8,128)} %collective-permute-done, pred[]{:T(512)S(6)} %eq.6, f32[2,1,128,512]{2,3,0,1:T(8,128)S(1)} %copy.17), kind=kLoop, calls=%fused_computation.19 | loop fusion | flops 262144 | bytes 2097153 | tf_op jit(solution)/shard_map/jit(_where)/select_n | solution.py:34
  37.4 0.1 copy.18
  37.5 23.6 %custom-call.7 = f32[2,128,128]{2,1,0:T(8,128)S(1)} custom-call(f32[2,128,128]{2,1,0:T(8,128)S(1)} %fusion.16), custom_call_target="Cholesky" | custom-call | tf_op jit(solution)/shard_map/jit(cholesky)/cholesky | solution.py:37
  61.1 0.8 select_reduce_fusion
  61.9 0.1 compare_reduce_fusion
  62.0 0.1 select_bitcast_fusion
  62.1 19.7 %custom-call.8 = f32[2,1,128,128]{2,3,1,0:T(8,128)S(1)} custom-call(f32[2,1,128,128]{3,2,1,0:T(8,128)S(1)} %select_bitcast_fusion), custom_call_target="InvertDiagBlocksLowerTriangular" | custom-call | tf_op jit(solution)/shard_map/triangular_solve | solution.py:15
  81.8 1.2 %fusion.14 = f32[2,128,128]{2,1,0:T(8,128)S(1)} fusion(f32[2,1,128,128]{2,3,1,0:T(8,128)S(1)} %custom-call.8, f32[128,128]{1,0:T(8,128)} %fusion.19), kind=kOutput, calls=%fused_computation.21 | convolution fusion | flops 50331648 | bytes 327680 | tf_op jit(solution)/shard_map/triangular_solve | solution.py:15
  83.1 0.8 fusion.6
  83.9 0.8 convolution_negate_fusion.1
  84.8 2.3 %fusion.4 = f32[2,48,768]{2,1,0:T(8,128)} fusion(f32[2,128,768]{2,1,0:T(8,128)S(1)} %convolution_negate_fusion.1, f32[2,48,384]{2,1,0:T(8,128)} %slice.54, pred[]{:T(512)S(6)} %eq.6, f32[2,48,512]{2,1,0:T(8,128)} %bitcast.38), kind=kOutput, calls=%fused_computation.8 | convolution fusion | flops 113393664 | bytes 1277953 | tf_op jit(solution)/shard_map/brs,bsc->brc/dot_general | solution.py:51
  87.0 0.0 collective-permute-done.1
  87.0 1.9 %fusion.10 = f32[2,128,768]{2,1,0:T(8,128)S(1)} fusion(f32[2,128,128]{2,1,0:T(8,128)S(1)} %fusion.14, f32[2,128,768]{2,1,0:T(8,128)S(1)} %fusion.12, f32[2,128,768]{2,1,0:T(8,128)} %collective-permute-done.1), kind=kOutput, calls=%fused_computation.14 | convolution fusion | flops 302186496 | bytes 2490368 | tf_op jit(solution)/shard_map/bij,bjq->biq/dot_general | solution.py:20
  89.0 0.8 fusion.3
  89.8 9.4 %fusion = bf16[2,2048,768]{2,1,0:T(8,128)(2,1)} fusion(f32[2,2048,768]{2,1,0:T(8,128)} %fusion.1, bf16[2,128,768]{2,1,0:T(8,128)(2,1)S(1)} %fusion.3, bf16[2,2048,512]{2,1,0:T(8,128)(2,1)} %param.5), kind=kOutput, calls=%fused_computation.1 | convolution fusion | flops 811597824 | bytes 20316160 | tf_op jit(solution)/shard_map/brs,bsq->brq/dot_general | solution.py:66
  (7 shorter events, 0.1 us)
Async XLA Ops:
  0.6 22.5 %copy-start = (bf16[2,3,128,768]{3,2,1,0:T(8,128)(2,1)S(1)}, bf16[2,3,128,768]{3,2,1,0:T(8,128)(2,1)}, u32[]{:S(2)}) copy-start(bf16[2,3,128,768]{3,2,1,0:T(8,128)(2,1)} %param.4) | copy-start | bytes 3538948
  0.6 25.0 %copy-start.2 = (f32[2,4,16,512]{3,2,1,0:T(8,128)S(1)}, f32[2,4,16,512]{3,2,1,0:T(8,128)}, u32[]{:S(2)}) copy-start(f32[2,4,16,512]{3,2,1,0:T(8,128)} %param.3) | copy-start | bytes 786436
  21.9 14.4 %collective-permute-start = (f32[2,128,512]{1,2,0:T(8,128)S(1)}, f32[2,128,512]{1,2,0:T(8,128)}, u32[]{:S(2)}, u32[]{:S(2)}) collective-permute-start(f32[2,128,512]{1,2,0:T(8,128)S(1)} %bitcast.35), channel_id=1, source_target_pairs={{0,8},{8,0},{16,24},{24,16},{32,40},{40,32},{48,56},{56,48},{64,72... | collective-permute-start | bytes 1572872 | tf_op jit(solution)/shard_map/ppermute | solution.py:10
  24.0 63.0 %collective-permute-start.1 = (f32[2,128,768]{2,1,0:T(8,128)S(1)}, f32[2,128,768]{2,1,0:T(8,128)}, u32[]{:S(2)}, u32[]{:S(2)}) collective-permute-start(f32[2,128,768]{2,1,0:T(8,128)S(1)} %fusion.12), channel_id=1, source_target_pairs={{0,8},{8,0},{16,24},{24,16},{32,40},{40,32},{48,56},{56,48},{64,72... | collective-permute-start | bytes 2359304 | tf_op jit(solution)/shard_map/ppermute | solution.py:10
  25.6 10.6 %copy-start.1 = (f32[2,3,16,512]{3,2,1,0:T(8,128)}, f32[2,3,16,512]{3,2,1,0:T(8,128)S(1)}, u32[]{:S(2)}) copy-start(f32[2,3,16,512]{3,2,1,0:T(8,128)S(1)} %slice.43) | copy-start | bytes 589828
where the time goes:
time: 99.6 us; the launch traced here: 99.2 us
  other arithmetic  46.7 us (47%)
  matrix products  28.1 us (28%)
  blocking collectives  20 us (20%)
  local copies, waits for them, and re-layouts  2.1 us (2%)
  starting transfers between devices  1.63 us (2%)
    another operation x4, other arithmetic, per_device(): factor = jnp.linalg.cholesky(shared_block)  25.1 us
    all_gather x1, blocking collectives, per_device(): own_edge = lax.all_gather(own_local, 'row', axis=1, tiled=True)  20 us
    another operation x3, other arithmetic, invert_factor(): lax.linalg.triangular_solve(factor, identity, left_side=True, lower=True)  19.8 us
    dot_general x1, matrix products, per_device(): jnp.einsum('bro,boq->brq', solution_op[:, :, :outer_size], own_data, pref...  9.88 us
    dot_general x1, matrix products, per_device(): jnp.einsum('brs,bsq->brq', solution_op[:, :, outer_size:], edge_values, p...  9.42 us
    dot_general x2, matrix products, solve_shared(): jnp.einsum('bij,bjq->biq', inverse_factor, right_side, precision=highest)  2.72 us
    dot_general x1, matrix products, per_device(): jnp.einsum('brs,bsc->brc', local_rows[:, :, outer_size:], transfer, preci...  2.28 us
  transfers between devices with their start and end apart: 2, of which 0 were waited for; matrix products, arithmetic and copies ran while one was open for 64% of the time, Pallas kernels for 0%

commit v1 on v0

v1 whole, which is shorter than its diff:
```python
import functools

import jax
import jax.numpy as jnp
from jax import lax
from jax.experimental import pallas as pl
from jax.experimental.pallas import tpu as pltpu
from jax.sharding import PartitionSpec as P

HIGHEST = lax.Precision.HIGHEST
F32 = jnp.float32
BF16 = jnp.bfloat16
REMAINDER = 2.0**-27
MOST_DOUBLINGS = 40


def from_partner(value):
    pairs = [(source, source ^ 1) for source in range(lax.axis_size("box"))]
    return lax.ppermute(value, "box", pairs)


def dot(left, right, precision=None):
    return jnp.dot(left, right, precision=precision, preferred_element_type=F32)


def invert_kernel(edge, side_ref, gathered_ref, map_ref, inverse_ref, parent_ref, sums, powers):
    boxes = inverse_ref.shape[0]
    outer = 3 * edge
    row = lax.broadcasted_iota(jnp.int32, (edge, edge), 0)
    column = lax.broadcasted_iota(jnp.int32, (edge, edge), 1)
    diagonal = row == column
    norm = jnp.zeros((1, 1), F32)
    for b in range(boxes):
        shared = gathered_ref[:, b, :, :edge].reshape(edge, edge)
        kept = jnp.where(diagonal, shared, 0.0)
        scale = 1.0 / jnp.sum(kept, axis=1, keepdims=True)
        power = jnp.where(diagonal, 0.0, -shared) * scale
        norm = jnp.maximum(norm, jnp.max(jnp.sum(jnp.abs(power), axis=1, keepdims=True), axis=0, keepdims=True))
        sums[b] = jnp.where(diagonal, 1.0, 0.0)
        powers[b] = power

    def more(carry):
        bound, count = carry
        return jnp.logical_and(bound > REMAINDER, count < MOST_DOUBLINGS)

    def square(carry):
        bound, count = carry
        return bound * bound, count + 1

    _, doublings = lax.while_loop(more, square, (norm[0, 0], jnp.int32(0)))

    def double(_, carry):
        for b in range(boxes):
            power = powers[b]
            both = dot(jnp.concatenate([sums[b], power], axis=0), power, HIGHEST)
            sums[b] = sums[b] + both[:edge]
            powers[b] = both[edge:]
        return carry

    lax.fori_loop(0, doublings, double, 0)
    is_alpha = side_ref[0] == 0
    for b in range(boxes):
        shared = gathered_ref[:, b, :, :edge].reshape(edge, edge)
        scale = 1.0 / jnp.sum(jnp.where(diagonal, shared, 0.0), axis=0, keepdims=True)
        inverse = sums[b] * scale
        inverse_ref[b] = inverse
        rows = map_ref[b, :3].reshape(-1, 4 * edge)
        weights = dot(rows[:, outer:], inverse, HIGHEST)
        coupling = gathered_ref[:, b, :, edge:].reshape(edge, 2 * outer)
        change = dot(weights, coupling, HIGHEST)
        own = (rows[:, :outer] - change[:, :outer]).reshape(3, -1, outer)
        other = (-change[:, outer:]).reshape(3, -1, outer)

        @pl.when(is_alpha)
        def _():
            parent_ref[b, :, :, :outer] = own
            parent_ref[b, :, :, outer:] = other

        @pl.when(jnp.logical_not(is_alpha))
        def _():
            parent_ref[b, :, :, :outer] = other
            parent_ref[b, :, :, outer:] = own


def split_three(value):
    first = value.astype(BF16)
    rest = value - first.astype(F32)
    second = rest.astype(BF16)
    third = (rest - second.astype(F32)).astype(BF16)
    return jnp.concatenate([first, second, third], axis=0)


def field_kernel(edge, gathered_ref, inverse_ref, own_ref, other_ref, operator_ref, field_ref, pressure):
    outer = 3 * edge

    @pl.when(pl.program_id(1) == 0)
    def _():
        own = own_ref[0]
        coupling = gathered_ref[:, 0, :, edge:].reshape(edge, 2 * outer)
        parts = dot(split_three(coupling[:, :outer]), own)
        parts += dot(split_three(coupling[:, outer:]), other_ref[0])
        terms = parts[:edge] + (parts[edge : 2 * edge] + parts[2 * edge :])
        pressure[:outer] = own
        pressure[outer:] = (-dot(inverse_ref[0], terms, HIGHEST)).astype(BF16)

    field_ref[0] = dot(operator_ref[0], pressure[...]).astype(BF16)


def per_device(dtn_map, boundary_data, solution_op):
    boxes, _, local, points = dtn_map.shape
    edge = boundary_data.shape[2]
    loads = boundary_data.shape[3]
    cells = solution_op.shape[1]
    outer = 3 * edge
    side = (lax.axis_index("box") % 2).astype(jnp.int32).reshape(1)
    own_rows = dtn_map[:, 3]
    own_data = boundary_data.reshape(boxes, outer, loads)
    other_rows = from_partner(own_rows)
    own_data, started = lax.optimization_barrier((own_data, own_rows))
    other_data = from_partner(own_data)
    packed = jnp.concatenate(
        [
            own_rows[:, :, outer:] + other_rows[:, :, outer:],
            own_rows[:, :, :outer],
            other_rows[:, :, :outer],
        ],
        axis=2,
    )
    gathered = lax.all_gather(packed, "row", axis=0)
    inverse, parent_map = pl.pallas_call(
        functools.partial(invert_kernel, edge),
        out_shape=(
            jax.ShapeDtypeStruct((boxes, edge, edge), F32),
            jax.ShapeDtypeStruct((boxes, 3, local, 2 * outer), F32),
        ),
        in_specs=[
            pl.BlockSpec(memory_space=pltpu.SMEM),
            pl.BlockSpec(memory_space=pltpu.VMEM),
            pl.BlockSpec(memory_space=pltpu.VMEM),
        ],
        out_specs=(
            pl.BlockSpec(memory_space=pltpu.VMEM),
            pl.BlockSpec(memory_space=pltpu.VMEM),
        ),
        scratch_shapes=[
            pltpu.VMEM((boxes, edge, edge), F32),
            pltpu.VMEM((boxes, edge, edge), F32),
        ],
        compiler_params=pltpu.CompilerParams(vmem_limit_bytes=16 << 20),
        name="invert",
    )(side, gathered, dtn_map)
    step = 512
    groups = gathered.shape[0]
    interior_field = pl.pallas_call(
        functools.partial(field_kernel, edge),
        grid=(boxes, cells // step),
        out_shape=jax.ShapeDtypeStruct((boxes, cells, loads), BF16),
        in_specs=[
            pl.BlockSpec((groups, 1, local, gathered.shape[3]), lambda b, i: (0, b, 0, 0)),
            pl.BlockSpec((1, edge, edge), lambda b, i: (b, 0, 0)),
            pl.BlockSpec((1, outer, loads), lambda b, i: (b, 0, 0)),
            pl.BlockSpec((1, outer, loads), lambda b, i: (b, 0, 0)),
            pl.BlockSpec((1, step, points), lambda b, i: (b, i, 0)),
        ],
        out_specs=pl.BlockSpec((1, step, loads), lambda b, i: (b, i, 0)),
        scratch_shapes=[pltpu.VMEM((points, loads), BF16)],
        compiler_params=pltpu.CompilerParams(vmem_limit_bytes=32 << 20),
        name="field",
    )(gathered, inverse, own_data, other_data, solution_op)
    return (parent_map, interior_field)


def solution(mesh):
    in_specs = (P("box", None, "row", None), P("box", None, None, None), P("box", "row", None))
    out_specs = (P("box", None, "row", None), P("box", "row", None))
    return jax.shard_map(
        per_device, mesh=mesh, in_specs=in_specs, out_specs=out_specs, check_vma=False
    )
```

time: 99.6 us -> 70.4 us (0.71)
  other arithmetic: 46.7 us -> 0.02 us
  matrix products: 28.1 us -> 0 us
  waiting for transfers between devices: 0.01 us -> 25.9 us
  Pallas kernels: 0 us -> 12.9 us
  blocking collectives: 20 us -> 23.3 us
  local copies, waits for them, and re-layouts: 2.1 us -> 5.27 us
    another operation x7 -> x0, other arithmetic: 44.9 us -> none  [the longest x4 25.1 us: per_device(): factor = jnp.linalg.cholesky(shared_block)]
    dot_general x8 -> x0, matrix products: 26.8 us -> none  [the longest x1 9.88 us: per_device(): jnp.einsum('bro,boq->brq', solution_op[:, :, :outer_size], own_data, pref...]
    ppermute x2, waiting for transfers between devices: 0.01 us -> 25.9 us  [from_partner(): return lax.ppermute(value, 'box', pairs)]
    pallas_call x0 -> x2, Pallas kernels: none -> 12.9 us  [the longest x1 8.89 us: per_device(): pl.pallas_call(functools.partial(field_kernel, edge), grid=(boxes, cells...]
    unnamed x7 -> x6, local copies, waits for them, and re-layouts: 0.07 us -> 4.41 us
    all_gather x1, blocking collectives: 20 us -> 23.3 us  [per_device(): gathered = lax.all_gather(packed, 'row', axis=0)]
    slice x5 -> x2, local copies, waits for them, and re-layouts: 1.72 us -> 0.01 us  [the longest x1 0.01 us: per_device(): own_rows[:, :, :outer]]
    another operation x1 -> x0, matrix products: 1.23 us -> none  [invert_factor(): lax.linalg.triangular_solve(factor, identity, left_side=True, lower=True)]
  transfers between devices with their start and end apart: 2 -> 2, of which waited for: 0 -> 1; matrix products, arithmetic and copies ran while one was open for 64% -> 0% of each run, Pallas kernels for 0% -> 6%
where the time goes in v1:
time: 70.4 us; the launch traced here: 70.2 us
  waiting for transfers between devices  25.9 us (37%)
  blocking collectives  23.3 us (33%)
  Pallas kernels  12.9 us (18%)
  local copies, waits for them, and re-layouts  5.27 us (7%)
  starting transfers between devices  2.13 us (3%)
    ppermute x2, waiting for transfers between devices, from_partner(): return lax.ppermute(value, 'box', pairs)  25.9 us
    all_gather x1, blocking collectives, per_device(): gathered = lax.all_gather(packed, 'row', axis=0)  23.3 us
    pallas_call x1, Pallas kernels, per_device(): pl.pallas_call(functools.partial(field_kernel, edge), grid=(boxes, cells...  8.89 us
    unnamed x6, local copies, waits for them, and re-layouts  4.41 us
    pallas_call x1, Pallas kernels, per_device(): pl.pallas_call(functools.partial(invert_kernel, edge), out_shape=(jax.Sha...  4.03 us
    ppermute x2, starting transfers between devices, from_partner(): return lax.ppermute(value, 'box', pairs)  2.13 us
  transfers between devices with their start and end apart: 2, of which 1 were waited for; matrix products, arithmetic and copies ran while one was open for 0% of the time, Pallas kernels for 6%

profile of v1, /device:TPU:1, one launch (start us, length us, event | category | flops | bytes accessed | tf_op | source)
XLA Modules:
  0.0 70.2 jit_solution(15781432432579789145)
XLA Ops:
  0.6 0.9 %slice_bitcast_fusion = f32[2,16,512]{2,1,0:T(8,128)S(1)} fusion(f32[2,4,16,512]{3,2,1,0:T(8,128)} %map_ref.1), kind=kLoop, calls=%fused_computation.1 | loop fusion | bytes 131072 | tf_op jit(solution)/shard_map/squeeze | solution.py:116
  1.5 2.0 %collective-permute-start.1 = (bf16[2,384,768]{2,1,0:T(8,128)(2,1)}, bf16[2,384,768]{2,1,0:T(8,128)(2,1)S(1)}, u32[]{:S(2)}, u32[]{:S(2)}) collective-permute-start(bf16[2,384,768]{2,1,0:T(8,128)(2,1)} %bitcast.9), channel_id=1, source_target_pairs={{0,8},{8,0},{16,24},{24,16},{32,40},{40,32},{48,56},{56,48},{64,72... | collective-permute-start | bytes 3538952 | tf_op jit(solution)/shard_map/ppermute | solution.py:19
  3.5 0.1 collective-permute-start
  3.6 25.9 %collective-permute-done = f32[2,16,512]{2,1,0:T(8,128)S(1)} collective-permute-done((f32[2,16,512]{2,1,0:T(8,128)S(1)}, f32[2,16,512]{2,1,0:T(8,128)S(1)}, u32[]{:S(2)}, u32[]{:S(2)}) %collective-permute-start) | collective-permute-done | bytes 65568 | tf_op jit(solution)/shard_map/ppermute | solution.py:19
  29.5 23.3 %all-gather = f32[16,16,896]{2,1,0:T(8,128)S(1)} all-gather(f32[2,16,896]{2,1,0:T(8,128)S(1)} %pad_maximum_fusion), channel_id=2, replica_groups=mesh['box'=32,'row'=8] {'row'}, dimensions={0}, use_global_device_ids=true | all-gather | bytes 1032192 | tf_op jit(solution)/shard_map/all_gather | solution.py:129
  52.8 0.0 copy-start.2
  52.8 0.9 %copy-done.2 = f32[2,4,16,512]{3,2,1,0:T(8,128)S(1)} copy-done((f32[2,4,16,512]{3,2,1,0:T(8,128)S(1)}, f32[2,4,16,512]{3,2,1,0:T(8,128)}, u32[]{:S(2)}) %copy-start.2) | copy-done | bytes 262168
  53.8 4.0 %invert.1 = (f32[2,128,128]{2,1,0:T(8,128)S(1)}, f32[2,3,16,768]{3,2,1,0:T(8,128)}) custom-call(s32[1]{0:T(128)} %bitcast.side_ref, f32[8,2,16,896]{3,2,1,0:T(8,128)S(1)} %bitcast.7, f32[2,4,16,512]{3,2,1,0:T(8,128)S(1)} %copy-done.2), custom_call_target="tpu_custom_call" | custom-call | tf_op jit(solution)/shard_map/invert/pallas_call | solution.py:130
  57.8 0.0 collective-permute-done.1.other_ref
  57.8 0.0 copy-start
  57.8 2.2 %copy-done = bf16[2,2048,512]{2,1,0:T(8,128)(2,1)S(1)} copy-done((bf16[2,2048,512]{2,1,0:T(8,128)(2,1)S(1)}, bf16[2,2048,512]{2,1,0:T(8,128)(2,1)}, u32[]{:S(2)}) %copy-start) | copy-done | bytes 4194328
  60.0 0.0 copy-start.1
  60.0 1.3 %copy-done.1 = bf16[2,3,128,768]{3,2,1,0:T(8,128)(2,1)S(1)} copy-done((bf16[2,3,128,768]{3,2,1,0:T(8,128)(2,1)S(1)}, bf16[2,3,128,768]{3,2,1,0:T(8,128)(2,1)}, u32[]{:S(2)}) %copy-start.1) | copy-done | bytes 1179672
  61.3 8.9 %field.1 = bf16[2,2048,768]{2,1,0:T(8,128)(2,1)} custom-call(f32[8,2,16,896]{3,2,1,0:T(8,128)S(1)} %bitcast.8, f32[2,128,128]{2,1,0:T(8,128)S(1)} %get-tuple-element.6.inverse_ref, bf16[2,384,768]{2,1,0:T(8,128)(2,1)S(1)} %bitcast.10, bf16[2,384,768]{2,1,0:T(8,128)(2,1)S(1)} %collective-permute-done.1.other_ref, bf16[2,2048,512]{2,1,0:T(8,128)(2,1)S(1)} %copy-done), custom_call_target="tpu_custom_call" | custom-call | tf_op jit(solution)/shard_map/field/pallas_call | solution.py:154
  (4 shorter events, 0.0 us)
Async XLA Ops:
  1.5 56.3 %collective-permute-start.1 = (bf16[2,384,768]{2,1,0:T(8,128)(2,1)}, bf16[2,384,768]{2,1,0:T(8,128)(2,1)S(1)}, u32[]{:S(2)}, u32[]{:S(2)}) collective-permute-start(bf16[2,384,768]{2,1,0:T(8,128)(2,1)} %bitcast.9), channel_id=1, source_target_pairs={{0,8},{8,0},{16,24},{24,16},{32,40},{40,32},{48,56},{56,48},{64,72... | collective-permute-start | bytes 3538952 | tf_op jit(solution)/shard_map/ppermute | solution.py:19
  3.5 26.0 %collective-permute-start = (f32[2,16,512]{2,1,0:T(8,128)S(1)}, f32[2,16,512]{2,1,0:T(8,128)S(1)}, u32[]{:S(2)}, u32[]{:S(2)}) collective-permute-start(f32[2,16,512]{2,1,0:T(8,128)S(1)} %slice_bitcast_fusion), channel_id=1, source_target_pairs={{0,8},{8,0},{16,24},{24,16},{32,40},{40,32},{48,56},{56,48},{64,72... | collective-permute-start | bytes 196616 | tf_op jit(solution)/shard_map/ppermute | solution.py:19
  52.8 1.0 %copy-start.2 = (f32[2,4,16,512]{3,2,1,0:T(8,128)S(1)}, f32[2,4,16,512]{3,2,1,0:T(8,128)}, u32[]{:S(2)}) copy-start(f32[2,4,16,512]{3,2,1,0:T(8,128)} %map_ref.1) | copy-start | bytes 786436
  57.8 2.2 %copy-start = (bf16[2,2048,512]{2,1,0:T(8,128)(2,1)S(1)}, bf16[2,2048,512]{2,1,0:T(8,128)(2,1)}, u32[]{:S(2)}) copy-start(bf16[2,2048,512]{2,1,0:T(8,128)(2,1)} %operator_ref.1) | copy-start | bytes 12582916
  60.0 1.3 %copy-start.1 = (bf16[2,3,128,768]{3,2,1,0:T(8,128)(2,1)S(1)}, bf16[2,3,128,768]{3,2,1,0:T(8,128)(2,1)}, u32[]{:S(2)}) copy-start(bf16[2,3,128,768]{3,2,1,0:T(8,128)(2,1)} %param.4) | copy-start | bytes 3538948

commit v2 on v1

--- a/solution.py
+++ b/solution.py
@@ -14,16 +14,16 @@
 MOST_DOUBLINGS = 40
 
 
-def from_partner(value):
-    pairs = [(source, source ^ 1) for source in range(lax.axis_size("box"))]
-    return lax.ppermute(value, "box", pairs)
+def exchange(value, axis):
+    pairs = [(source, source ^ 1) for source in range(lax.axis_size(axis))]
+    return lax.ppermute(value, axis, pairs)
 
 
 def dot(left, right, precision=None):
     return jnp.dot(left, right, precision=precision, preferred_element_type=F32)
 
 
-def invert_kernel(edge, side_ref, gathered_ref, map_ref, inverse_ref, parent_ref, sums, powers):
+def invert_kernel(edge, place_ref, gathered_ref, map_ref, inverse_ref, parent_ref, sums, powers):
     boxes = inverse_ref.shape[0]
     outer = 3 * edge
     row = lax.broadcasted_iota(jnp.int32, (edge, edge), 0)
@@ -58,7 +58,7 @@
         return carry
 
     lax.fori_loop(0, doublings, double, 0)
-    is_alpha = side_ref[0] == 0
+    is_alpha = place_ref[0] < 2
     for b in range(boxes):
         shared = gathered_ref[:, b, :, :edge].reshape(edge, edge)
         scale = 1.0 / jnp.sum(jnp.where(diagonal, shared, 0.0), axis=0, keepdims=True)
@@ -90,20 +90,96 @@
     return jnp.concatenate([first, second, third], axis=0)
 
 
-def field_kernel(edge, gathered_ref, inverse_ref, own_ref, other_ref, operator_ref, field_ref, pressure):
+def early_kernel(chunk, place_ref, rows_ref, data_ref, operator_ref, partial_ref, sent_ref, staged, arrived):
+    boxes, cells, _ = partial_ref.shape
+    depth = staged.shape[2]
+    places = [(b, slice(start, start + chunk)) for b in range(boxes) for start in range(0, cells, chunk)]
+    copies = [
+        pltpu.make_async_copy(
+            operator_ref.at[b, cut, pl.ds(0, depth)], staged.at[b, cut], arrived.at[order]
+        )
+        for order, (b, cut) in enumerate(places)
+    ]
+    for copy in copies:
+        copy.start()
+    sent_ref[...] = data_ref[place_ref[0] & 1]
+    for copy, (b, cut) in zip(copies, places):
+        copy.wait()
+        partial_ref[b, cut] = dot(staged[b, cut], data_ref[b, :depth])
+
+
+def field_kernel(
+    edge,
+    chunk,
+    place_ref,
+    gathered_ref,
+    inverse_ref,
+    own_ref,
+    crossed_ref,
+    sibling_ref,
+    partial_ref,
+    operator_ref,
+    field_ref,
+    staged,
+    pressure,
+    finished,
+    arrived,
+    left,
+):
+    boxes, cells, _ = partial_ref.shape
     outer = 3 * edge
-
-    @pl.when(pl.program_id(1) == 0)
-    def _():
-        own = own_ref[0]
-        coupling = gathered_ref[:, 0, :, edge:].reshape(edge, 2 * outer)
+    depth = staged.shape[2]
+    core = place_ref[0] & 1
+    order = [core if turn == 0 else 1 - core for turn in range(boxes)]
+    starts = range(0, cells, chunk)
+    count = len(starts)
+    reads = [
+        pltpu.make_async_copy(
+            operator_ref.at[order[turn], pl.ds(start, chunk), pl.ds(depth, depth)],
+            staged.at[turn, pl.ds(start, chunk)],
+            arrived.at[turn * count + place],
+        )
+        for turn in range(boxes)
+        for place, start in enumerate(starts)
+    ]
+    for copy in reads:
+        copy.start()
+    writes = []
+    for turn, other_ref in enumerate((crossed_ref, sibling_ref)):
+        b = order[turn]
+        own = own_ref[b]
+        coupling = gathered_ref[:, b, :, edge:].reshape(edge, 2 * outer)
         parts = dot(split_three(coupling[:, :outer]), own)
-        parts += dot(split_three(coupling[:, outer:]), other_ref[0])
+        parts += dot(split_three(coupling[:, outer:]), other_ref[...])
         terms = parts[:edge] + (parts[edge : 2 * edge] + parts[2 * edge :])
-        pressure[:outer] = own
-        pressure[outer:] = (-dot(inverse_ref[0], terms, HIGHEST)).astype(BF16)
-
-    field_ref[0] = dot(operator_ref[0], pressure[...]).astype(BF16)
+        pressure[: outer - depth] = own[depth:]
+        pressure[outer - depth :] = (-dot(inverse_ref[b], terms, HIGHEST)).astype(BF16)
+        for place, start in enumerate(starts):
+            reads[turn * count + place].wait()
+            cut = slice(start, start + chunk)
+            total = partial_ref[b, cut] + dot(staged[turn, cut], pressure[...])
+            finished[turn, cut] = total.astype(BF16)
+            copy = pltpu.make_async_copy(
+                finished.at[turn, cut], field_ref.at[b, cut], left.at[turn * count + place]
+            )
+            copy.start()
+            writes.append(copy)
+    for copy in writes:
+        copy.wait()
+
+
+def in_vmem(value):
+    return pltpu.with_memory_space_constraint(value, pltpu.VMEM)
+
+
+def in_hbm(value):
+    return pltpu.with_memory_space_constraint(value, pltpu.HBM)
+
+
+SMEM_SPEC = pl.BlockSpec(memory_space=pltpu.SMEM)
+VMEM_SPEC = pl.BlockSpec(memory_space=pltpu.VMEM)
+HBM_SPEC = pl.BlockSpec(memory_space=pltpu.HBM)
+ANY_SPEC = pl.BlockSpec(memory_space=pl.ANY)
 
 
 def per_device(dtn_map, boundary_data, solution_op):
@@ -112,12 +188,35 @@
     loads = boundary_data.shape[3]
     cells = solution_op.shape[1]
     outer = 3 * edge
-    side = (lax.axis_index("box") % 2).astype(jnp.int32).reshape(1)
+    depth = points // 2
+    side = lax.axis_index("box") & 1
+    core = lax.axis_index("row") & 1
+    place = (2 * side + core).astype(jnp.int32).reshape(1)
     own_rows = dtn_map[:, 3]
     own_data = boundary_data.reshape(boxes, outer, loads)
-    other_rows = from_partner(own_rows)
-    own_data, started = lax.optimization_barrier((own_data, own_rows))
-    other_data = from_partner(own_data)
+    operator = in_hbm(solution_op)
+    other_rows = exchange(own_rows, "box")
+    chunk = 512
+    pieces = boxes * cells // chunk
+    partial, sent = pl.pallas_call(
+        functools.partial(early_kernel, chunk),
+        out_shape=(
+            pltpu.VMEM((boxes, cells, loads), F32),
+            jax.ShapeDtypeStruct((outer, loads), BF16),
+        ),
+        in_specs=[SMEM_SPEC, ANY_SPEC, VMEM_SPEC, HBM_SPEC],
+        out_specs=(VMEM_SPEC, VMEM_SPEC),
+        scratch_shapes=[
+            pltpu.VMEM((boxes, cells, depth), BF16),
+            pltpu.SemaphoreType.DMA((pieces,)),
+        ],
+        compiler_params=pltpu.CompilerParams(vmem_limit_bytes=24 << 20),
+        cost_estimate=pl.CostEstimate(
+            flops=2 * boxes * cells * depth * loads, bytes_accessed=4 << 20, transcendentals=0
+        ),
+        name="early",
+    )(place, own_rows, own_data, operator)
+    crossed = exchange(sent, "box")
     packed = jnp.concatenate(
         [
             own_rows[:, :, outer:] + other_rows[:, :, outer:],
@@ -127,46 +226,39 @@
         axis=2,
     )
     gathered = lax.all_gather(packed, "row", axis=0)
+    crossed, gathered = lax.optimization_barrier((crossed, gathered))
+    sibling = exchange(crossed, "row")
     inverse, parent_map = pl.pallas_call(
         functools.partial(invert_kernel, edge),
         out_shape=(
             jax.ShapeDtypeStruct((boxes, edge, edge), F32),
             jax.ShapeDtypeStruct((boxes, 3, local, 2 * outer), F32),
         ),
-        in_specs=[
-            pl.BlockSpec(memory_space=pltpu.SMEM),
-            pl.BlockSpec(memory_space=pltpu.VMEM),
-            pl.BlockSpec(memory_space=pltpu.VMEM),
-        ],
-        out_specs=(
-            pl.BlockSpec(memory_space=pltpu.VMEM),
-            pl.BlockSpec(memory_space=pltpu.VMEM),
-        ),
+        in_specs=[SMEM_SPEC, VMEM_SPEC, VMEM_SPEC],
+        out_specs=(VMEM_SPEC, VMEM_SPEC),
         scratch_shapes=[
             pltpu.VMEM((boxes, edge, edge), F32),
             pltpu.VMEM((boxes, edge, edge), F32),
         ],
-        compiler_params=pltpu.CompilerParams(vmem_limit_bytes=16 << 20),
+        compiler_params=pltpu.CompilerParams(vmem_limit_bytes=8 << 20),
+        cost_estimate=pl.CostEstimate(flops=4 << 30, bytes_accessed=4 << 20, transcendentals=0),
         name="invert",
-    )(side, gathered, dtn_map)
-    step = 512
-    groups = gathered.shape[0]
+    )(place, gathered, dtn_map)
     interior_field = pl.pallas_call(
-        functools.partial(field_kernel, edge),
-        grid=(boxes, cells // step),
+        functools.partial(field_kernel, edge, chunk),
         out_shape=jax.ShapeDtypeStruct((boxes, cells, loads), BF16),
-        in_specs=[
-            pl.BlockSpec((groups, 1, local, gathered.shape[3]), lambda b, i: (0, b, 0, 0)),
-            pl.BlockSpec((1, edge, edge), lambda b, i: (b, 0, 0)),
-            pl.BlockSpec((1, outer, loads), lambda b, i: (b, 0, 0)),
-            pl.BlockSpec((1, outer, loads), lambda b, i: (b, 0, 0)),
-            pl.BlockSpec((1, step, points), lambda b, i: (b, i, 0)),
-        ],
-        out_specs=pl.BlockSpec((1, step, loads), lambda b, i: (b, i, 0)),
-        scratch_shapes=[pltpu.VMEM((points, loads), BF16)],
-        compiler_params=pltpu.CompilerParams(vmem_limit_bytes=32 << 20),
+        in_specs=[SMEM_SPEC] + [VMEM_SPEC] * 6 + [HBM_SPEC],
+        out_specs=ANY_SPEC,
+        scratch_shapes=[
+            pltpu.VMEM((boxes, cells, depth), BF16),
+            pltpu.VMEM((depth, loads), BF16),
+            pltpu.VMEM((boxes, cells, loads), BF16),
+            pltpu.SemaphoreType.DMA((pieces,)),
+            pltpu.SemaphoreType.DMA((pieces,)),
+        ],
+        compiler_params=pltpu.CompilerParams(vmem_limit_bytes=28 << 20),
         name="field",
-    )(gathered, inverse, own_data, other_data, solution_op)
+    )(place, gathered, inverse, own_data, crossed, sibling, in_vmem(partial), operator)
     return (parent_map, interior_field)
 
 

time: 70.4 us -> 42.4 us (0.60)
  waiting for transfers between devices: 25.9 us -> 0.01 us
  local copies, waits for them, and re-layouts: 5.27 us -> 2.14 us
  Pallas kernels: 12.9 us -> 15.3 us
  blocking collectives: 23.3 us -> 21.7 us
    ppermute x2 -> x3, waiting for transfers between devices: 25.9 us -> 0.01 us  [exchange(): return lax.ppermute(value, axis, pairs)]
    unnamed x6 -> x4, local copies, waits for them, and re-layouts: 4.41 us -> 1.27 us
    pallas_call x1 -> x2, Pallas kernels: 8.89 us -> 11.3 us  [the longest x1 6.81 us: per_device(): pl.pallas_call(functools.partial(field_kernel, edge, chunk), out_shape=ja...]
    all_gather x1, blocking collectives: 23.3 us -> 21.7 us  [per_device(): gathered = lax.all_gather(packed, 'row', axis=0)]
    ppermute x2 -> x3, starting transfers between devices: 2.13 us -> 2.3 us  [exchange(): return lax.ppermute(value, axis, pairs)]
  transfers between devices with their start and end apart: 2 -> 3, of which waited for: 1 -> 0; matrix products, arithmetic and copies ran while one was open for 0% -> 0% of each run, Pallas kernels for 6% -> 20%
where the time goes in v2:
time: 42.4 us; the launch traced here: 42.2 us
  blocking collectives  21.7 us (51%)
  Pallas kernels  15.3 us (36%)
  starting transfers between devices  2.3 us (5%)
  local copies, waits for them, and re-layouts  2.14 us (5%)
  between operations  0.69 us (2%)
    all_gather x1, blocking collectives, per_device(): gathered = lax.all_gather(packed, 'row', axis=0)  21.7 us
    pallas_call x1, Pallas kernels, per_device(): pl.pallas_call(functools.partial(field_kernel, edge, chunk), out_shape=ja...  6.81 us
    pallas_call x1, Pallas kernels, per_device(): pl.pallas_call(functools.partial(early_kernel, chunk), out_shape=(pltpu.V...  4.48 us
    pallas_call x1, Pallas kernels, per_device(): pl.pallas_call(functools.partial(invert_kernel, edge), out_shape=(jax.Sha...  4.03 us
    ppermute x3, starting transfers between devices, exchange(): return lax.ppermute(value, axis, pairs)  2.3 us
    unnamed x4, local copies, waits for them, and re-layouts  1.27 us
    squeeze x1, local copies, waits for them, and re-layouts, per_device(): own_rows = dtn_map[:, 3]  0.85 us
  transfers between devices with their start and end apart: 3, of which 0 were waited for; matrix products, arithmetic and copies ran while one was open for 0% of the time, Pallas kernels for 20%

profile of v2, /device:TPU:1, one launch (start us, length us, event | category | flops | bytes accessed | tf_op | source)
XLA Modules:
  0.0 42.2 jit_solution(12960243170538442202)
XLA Ops:
  0.6 0.9 %slice_bitcast_fusion.rows_ref = f32[2,16,512]{2,1,0:T(8,128)S(1)} fusion(f32[2,4,16,512]{3,2,1,0:T(8,128)} %map_ref.1), kind=kLoop, calls=%fused_computation.1 | loop fusion | bytes 131072 | tf_op jit(solution)/shard_map/squeeze | solution.py:195
  1.5 2.0 %collective-permute-start.1 = (f32[2,16,512]{2,1,0:T(8,128)S(1)}, f32[2,16,512]{2,1,0:T(8,128)S(1)}, u32[]{:S(2)}, u32[]{:S(2)}) collective-permute-start(f32[2,16,512]{2,1,0:T(8,128)S(1)} %slice_bitcast_fusion.rows_ref), channel_id=1, source_target_pairs={{0,8},{8,0},{16,24},{24,16},{32,40},{40,32},{48,56},{56,48},{64,72... | collective-permute-start | bytes 196616 | tf_op jit(solution)/shard_map/ppermute | solution.py:19
  3.5 0.0 copy-start
  3.5 1.3 %copy-done = bf16[2,3,128,768]{3,2,1,0:T(8,128)(2,1)S(1)} copy-done((bf16[2,3,128,768]{3,2,1,0:T(8,128)(2,1)S(1)}, bf16[2,3,128,768]{3,2,1,0:T(8,128)(2,1)}, u32[]{:S(2)}) %copy-start) | copy-done | bytes 1179672
  4.8 0.0 copy-start.1
  4.8 4.5 %early.1 = (f32[2,2048,768]{2,1,0:T(8,128)S(1)}, bf16[384,768]{1,0:T(8,128)(2,1)S(1)}) custom-call(s32[1]{0:T(128)} %bitcast.place_ref, f32[2,16,512]{2,1,0:T(8,128)S(1)} %slice_bitcast_fusion.rows_ref, bf16[2,384,768]{2,1,0:T(8,128)(2,1)S(1)} %bitcast.9, bf16[2,2048,512]{2,1,0:T(8,128)(2,1)} %operator_ref.3), custom_call_target="tpu_custom_call" | custom-call | flops 1610612736 | bytes 4194304 | tf_op jit(solution)/shard_map/early/pallas_call | solution.py:201
  9.3 0.1 collective-permute-start
  9.4 0.0 collective-permute-done.1
  9.5 21.7 %all-gather = f32[16,16,896]{2,1,0:T(8,128)S(1)} all-gather(f32[2,16,896]{2,1,0:T(8,128)S(1)} %pad_maximum_fusion), channel_id=2, replica_groups=mesh['box'=32,'row'=8] {'row'}, dimensions={0}, use_global_device_ids=true | all-gather | bytes 1032192 | tf_op jit(solution)/shard_map/all_gather | solution.py:228
  31.2 0.0 collective-permute-done.crossed_ref
  31.2 0.2 collective-permute-start.2
  31.3 0.0 copy-done.1
  31.3 4.0 %invert.1 = (f32[2,128,128]{2,1,0:T(8,128)S(1)}, f32[2,3,16,768]{3,2,1,0:T(8,128)}) custom-call(s32[1]{0:T(128)} %bitcast.place_ref, f32[8,2,16,896]{3,2,1,0:T(8,128)S(1)} %bitcast.7, f32[2,4,16,512]{3,2,1,0:T(8,128)S(1)} %copy-done.1), custom_call_target="tpu_custom_call" | custom-call | flops 4294967296 | bytes 4194304 | tf_op jit(solution)/shard_map/invert/pallas_call | solution.py:231
  35.4 0.0 collective-permute-done.2.sibling_ref
  35.4 6.8 %field.1 = bf16[2,2048,768]{2,1,0:T(8,128)(2,1)} custom-call(s32[1]{0:T(128)} %bitcast.place_ref, f32[8,2,16,896]{3,2,1,0:T(8,128)S(1)} %bitcast.8, f32[2,128,128]{2,1,0:T(8,128)S(1)} %get-tuple-element.11.inverse_ref, bf16[2,384,768]{2,1,0:T(8,128)(2,1)S(1)} %bitcast.10, bf16[384,768]{1,0:T(8,128)(2,1)S(1)} %collective-permute-done.crossed_ref, ...), custom_call_target="tpu_custom_call" | custom-call | tf_op jit(solution)/shard_map/field/pallas_call | solution.py:247
  (4 shorter events, 0.0 us)
Async XLA Ops:
  1.5 7.9 %collective-permute-start.1 = (f32[2,16,512]{2,1,0:T(8,128)S(1)}, f32[2,16,512]{2,1,0:T(8,128)S(1)}, u32[]{:S(2)}, u32[]{:S(2)}) collective-permute-start(f32[2,16,512]{2,1,0:T(8,128)S(1)} %slice_bitcast_fusion.rows_ref), channel_id=1, source_target_pairs={{0,8},{8,0},{16,24},{24,16},{32,40},{40,32},{48,56},{56,48},{64,72... | collective-permute-start | bytes 196616 | tf_op jit(solution)/shard_map/ppermute | solution.py:19
  3.5 1.3 %copy-start = (bf16[2,3,128,768]{3,2,1,0:T(8,128)(2,1)S(1)}, bf16[2,3,128,768]{3,2,1,0:T(8,128)(2,1)}, u32[]{:S(2)}) copy-start(bf16[2,3,128,768]{3,2,1,0:T(8,128)(2,1)} %param.4) | copy-start | bytes 3538948
  4.8 26.5 %copy-start.1 = (f32[2,4,16,512]{3,2,1,0:T(8,128)S(1)}, f32[2,4,16,512]{3,2,1,0:T(8,128)}, u32[]{:S(2)}) copy-start(f32[2,4,16,512]{3,2,1,0:T(8,128)} %map_ref.1) | copy-start | bytes 786436
  9.3 21.9 %collective-permute-start = (bf16[384,768]{1,0:T(8,128)(2,1)S(1)}, bf16[384,768]{1,0:T(8,128)(2,1)S(1)}, u32[]{:S(2)}, u32[]{:S(2)}) collective-permute-start(bf16[384,768]{1,0:T(8,128)(2,1)S(1)} %get-tuple-element.8), channel_id=1, source_target_pairs={{0,8},{8,0},{16,24},{24,16},{32,40},{40,32},{48,56},{56,48},{64,72... | collective-permute-start | bytes 1769480 | tf_op jit(solution)/shard_map/ppermute | solution.py:19
  31.2 4.2 %collective-permute-start.2 = (bf16[384,768]{1,0:T(8,128)(2,1)S(1)}, bf16[384,768]{1,0:T(8,128)(2,1)S(1)}, u32[]{:S(2)}, u32[]{:S(2)}) collective-permute-start(bf16[384,768]{1,0:T(8,128)(2,1)S(1)} %collective-permute-done.crossed_ref), channel_id=1, source_target_pairs={{0,1},{1,0},{2,3},{3,2},{4,5},{5,4},{6,7},{7,6},{8,9},{9,8},{10,11... | collective-permute-start | bytes 1769480 | tf_op jit(solution)/shard_map/ppermute | solution.py:19

commit v3 on v0

v3 whole, which is shorter than its diff:
```python
import functools

import jax
import jax.numpy as jnp
from jax import lax
from jax.experimental import pallas as pl
from jax.experimental.pallas import tpu as pltpu
from jax.sharding import PartitionSpec as P

HIGHEST = lax.Precision.HIGHEST
F32 = jnp.float32
BF16 = jnp.bfloat16
REMAINDER = 2.0**-27
SURE_DOUBLINGS = 4
MOST_DOUBLINGS = 40

SMEM_SPEC = pl.BlockSpec(memory_space=pltpu.SMEM)
VMEM_SPEC = pl.BlockSpec(memory_space=pltpu.VMEM)
HBM_SPEC = pl.BlockSpec(memory_space=pltpu.HBM)
ANY_SPEC = pl.BlockSpec(memory_space=pl.ANY)


def exchange(value, axis):
    pairs = [(source, source ^ 1) for source in range(lax.axis_size(axis))]
    return lax.ppermute(value, axis, pairs)


def dot(left, right, precision=None):
    return jnp.dot(left, right, precision=precision, preferred_element_type=F32)


def in_hbm(value):
    return pltpu.with_memory_space_constraint(value, pltpu.HBM)


def split(value, count):
    pieces = []
    for _ in range(count):
        piece = value.astype(BF16)
        pieces.append(piece)
        value = value - piece.astype(F32)
    return pieces


def split_dot(left, right):
    high, low = split(left, 2)
    right_high, right_low = split(right, 2)
    both = dot(jnp.concatenate([high, low], axis=0), right_high)
    rows = left.shape[0]
    return both[:rows] + (both[rows:] + dot(high, right_low))


def start_kernel(place_ref, map_ref, data_ref, rows_ref, first_ref, arrived):
    copies = (
        pltpu.make_async_copy(map_ref.at[:, 3], rows_ref, arrived.at[0]),
        pltpu.make_async_copy(data_ref.at[place_ref[0] & 1], first_ref, arrived.at[1]),
    )
    for copy in copies:
        copy.start()
    for copy in copies:
        copy.wait()


def early_kernel(
    chunk,
    place_ref,
    first_ref,
    rows_ref,
    map_ref,
    data_ref,
    operator_ref,
    sent_ref,
    outer_ref,
    second_ref,
    near_ref,
    far_ref,
    partial_ref,
    arrived,
):
    mine = place_ref[0] & 1
    cells, loads = partial_ref.shape
    depth = operator_ref.shape[2] // 2
    cuts = [slice(start, start + chunk) for start in range(0, cells, chunk)]
    moves = [(operator_ref.at[mine, cut], near_ref.at[cut]) for cut in cuts]
    moves += [(operator_ref.at[1 - mine, cut], far_ref.at[cut]) for cut in cuts]
    moves += [(data_ref.at[1 - mine], second_ref), (map_ref.at[:, pl.ds(0, 3)], outer_ref)]
    copies = [
        pltpu.make_async_copy(origin, target, arrived.at[order])
        for order, (origin, target) in enumerate(moves)
    ]
    for copy in copies:
        copy.start()
    for copy, cut in zip(copies, cuts):
        copy.wait()
        partial_ref[cut] = dot(near_ref[cut, :depth], first_ref[:depth])
    for copy in copies[len(cuts) :]:
        copy.wait()


def solve_kernel(place_ref, gathered_ref, own_ref, other_ref, solved_ref, sums, power_ref):
    mine = place_ref[0] & 1
    edge = sums.shape[0]
    outer, loads = own_ref.shape
    shared = gathered_ref[:, mine, :, :edge].reshape(edge, edge)
    row = lax.broadcasted_iota(jnp.int32, (edge, edge), 0)
    column = lax.broadcasted_iota(jnp.int32, (edge, edge), 1)
    diagonal = row == column
    kept = jnp.where(diagonal, shared, 0.0)
    scale = 1.0 / jnp.sum(kept, axis=1, keepdims=True)
    right_scale = 1.0 / jnp.sum(kept, axis=0, keepdims=True)
    power = jnp.where(diagonal, 0.0, -shared) * scale
    size = jnp.sum(jnp.abs(power), axis=1, keepdims=True)
    norm = jnp.max(size, axis=0, keepdims=True)[0, 0]

    coupling = gathered_ref[:, mine, :, edge:].reshape(edge, 2 * outer)
    parts = dot(jnp.concatenate(split(coupling[:, :outer], 3), axis=0), own_ref[...])
    parts += dot(jnp.concatenate(split(coupling[:, outer:], 3), axis=0), other_ref[...])
    terms = parts[:edge] + (parts[edge : 2 * edge] + parts[2 * edge :])

    total = jnp.where(diagonal, 1.0, power)
    power = dot(power, power, HIGHEST)
    for _ in range(SURE_DOUBLINGS - 1):
        both = dot(jnp.concatenate([total, power], axis=0), power, HIGHEST)
        total = total + both[:edge]
        power = both[edge:]
    sums[...] = total + dot(total, power, HIGHEST)

    bound = norm
    for _ in range(SURE_DOUBLINGS + 1):
        bound = bound * bound

    @pl.when(bound > REMAINDER)
    def _():
        power_ref[...] = dot(power, power, HIGHEST)

        def more(carry):
            left, count = carry
            return jnp.logical_and(left > REMAINDER, count < MOST_DOUBLINGS)

        def double(carry):
            left, count = carry
            held = power_ref[...]
            both = dot(jnp.concatenate([sums[...], held], axis=0), held, HIGHEST)
            sums[...] = sums[...] + both[:edge]
            power_ref[...] = both[edge:]
            return left * left, count + 1

        lax.while_loop(more, double, (bound, jnp.int32(0)))

    inverse = sums[...] * right_scale
    solved_ref[:, :loads] = (-split_dot(inverse, terms)).astype(BF16)
    for order, piece in enumerate(split(inverse, 3)):
        solved_ref[:, loads + order * edge : loads + (order + 1) * edge] = piece


def field_kernel(turn, chunk, place_ref, gathered_ref, map_ref, solved_ref, data_ref, operator_ref, *refs):
    if turn:
        refs = refs[2:]
    else:
        partial_ref, *refs = refs
    field_ref, parent_ref, pressure, finished, parent, left = refs
    box = place_ref[0] & 1
    if turn:
        box = 1 - box
    outer, loads = data_ref.shape
    edge = solved_ref.shape[0]
    cells, points = operator_ref.shape
    done = 0 if turn else points // 2
    pressure[:outer] = data_ref[...]
    pressure[outer:] = solved_ref[:, :loads]
    writes = []
    for order, start in enumerate(range(0, cells, chunk)):
        cut = slice(start, start + chunk)
        total = dot(operator_ref[cut, done:], pressure[done:])
        if not turn:
            total = total + partial_ref[cut]
        finished[cut] = total.astype(BF16)
        copy = pltpu.make_async_copy(finished.at[cut], field_ref.at[box, cut], left.at[order])
        copy.start()
        writes.append(copy)
    inverse = jnp.zeros((edge, edge), F32)
    for order in (2, 1, 0):
        inverse = inverse + solved_ref[:, loads + order * edge : loads + (order + 1) * edge].astype(F32)
    rows = map_ref[box].reshape(-1, 4 * edge)
    weights = split_dot(rows[:, outer:], inverse)
    coupling = gathered_ref[:, box, :, edge:].reshape(edge, 2 * outer)
    change = split_dot(weights, coupling)
    own = (rows[:, :outer] - change[:, :outer]).reshape(3, -1, outer)
    other = (-change[:, outer:]).reshape(3, -1, outer)
    is_alpha = place_ref[0] < 2

    @pl.when(is_alpha)
    def _():
        parent[:, :, :outer] = own
        parent[:, :, outer:] = other

    @pl.when(jnp.logical_not(is_alpha))
    def _():
        parent[:, :, :outer] = other
        parent[:, :, outer:] = own

    copy = pltpu.make_async_copy(parent, parent_ref.at[box], left.at[len(writes)])
    copy.start()
    writes.append(copy)
    for copy in writes:
        copy.wait()


def per_device(dtn_map, boundary_data, solution_op):
    boxes, _, local, points = dtn_map.shape
    edge = boundary_data.shape[2]
    loads = boundary_data.shape[3]
    cells = solution_op.shape[1]
    outer = 3 * edge
    side = lax.axis_index("box") & 1
    core = lax.axis_index("row") & 1
    place = (2 * side + core).astype(jnp.int32).reshape(1)
    whole_map = in_hbm(dtn_map)
    data = in_hbm(boundary_data.reshape(boxes, outer, loads))
    half = jax.ShapeDtypeStruct((outer, loads), BF16)
    own_rows, first = pl.pallas_call(
        start_kernel,
        out_shape=(jax.ShapeDtypeStruct((boxes, local, points), F32), half),
        in_specs=[SMEM_SPEC, HBM_SPEC, HBM_SPEC],
        out_specs=(VMEM_SPEC, VMEM_SPEC),
        scratch_shapes=[pltpu.SemaphoreType.DMA((2,))],
        compiler_params=pltpu.CompilerParams(vmem_limit_bytes=4 << 20),
        name="start",
    )(place, whole_map, data)
    other_rows = exchange(own_rows, "box")
    chunk = 512
    sent, outer_rows, second, near, far, partial = pl.pallas_call(
        functools.partial(early_kernel, chunk),
        out_shape=(
            half,
            pltpu.VMEM((boxes, 3, local, points), F32),
            pltpu.VMEM((outer, loads), BF16),
            pltpu.VMEM((cells, points), BF16),
            pltpu.VMEM((cells, points), BF16),
            pltpu.VMEM((cells, loads), F32),
        ),
        in_specs=[SMEM_SPEC, VMEM_SPEC, ANY_SPEC, HBM_SPEC, HBM_SPEC, HBM_SPEC],
        out_specs=(VMEM_SPEC,) * 6,
        scratch_shapes=[pltpu.SemaphoreType.DMA((2 * cells // chunk + 2,))],
        input_output_aliases={1: 0},
        compiler_params=pltpu.CompilerParams(vmem_limit_bytes=4 << 20),
        cost_estimate=pl.CostEstimate(
            flops=cells * points * loads, bytes_accessed=6 << 20, transcendentals=0
        ),
        name="early",
    )(place, first, own_rows, whole_map, data, in_hbm(solution_op))
    first = sent
    crossed = exchange(sent, "box")
    packed = jnp.concatenate(
        [
            own_rows[:, :, outer:] + other_rows[:, :, outer:],
            own_rows[:, :, :outer],
            other_rows[:, :, :outer],
        ],
        axis=2,
    )
    gathered = lax.all_gather(packed, "row", axis=0)
    solved = pl.pallas_call(
        solve_kernel,
        out_shape=jax.ShapeDtypeStruct((edge, loads + 3 * edge), BF16),
        in_specs=[SMEM_SPEC] + [VMEM_SPEC] * 3,
        out_specs=VMEM_SPEC,
        scratch_shapes=[pltpu.VMEM((edge, edge), F32), pltpu.VMEM((edge, edge), F32)],
        compiler_params=pltpu.CompilerParams(vmem_limit_bytes=12 << 20),
        name="solve",
    )(place, gathered, first, crossed)
    swapped = exchange(solved, "row")
    outputs = (
        jax.ShapeDtypeStruct((boxes, cells, loads), BF16),
        jax.ShapeDtypeStruct((boxes, 3, local, 2 * outer), F32),
    )

    def field(turn, given, data, operator, extra):
        return pl.pallas_call(
            functools.partial(field_kernel, turn, chunk),
            out_shape=outputs,
            in_specs=[SMEM_SPEC] + [VMEM_SPEC] * 5 + ([ANY_SPEC] * 2 if turn else [VMEM_SPEC]),
            out_specs=(ANY_SPEC, ANY_SPEC),
            scratch_shapes=[
                pltpu.VMEM((points, loads), BF16),
                pltpu.VMEM((cells, loads), BF16),
                pltpu.VMEM((3, local, 2 * outer), F32),
                pltpu.SemaphoreType.DMA((cells // chunk + 1,)),
            ],
            input_output_aliases={6: 0, 7: 1} if turn else {},
            compiler_params=pltpu.CompilerParams(vmem_limit_bytes=16 << 20),
            cost_estimate=pl.CostEstimate(
                flops=2 * cells * points * loads, bytes_accessed=8 << 20, transcendentals=0
            ),
            name="field",
        )(place, gathered, outer_rows, given, data, operator, *extra)

    made = field(0, solved, first, near, (partial,))
    interior_field, parent_map = field(1, swapped, second, far, made)
    return (parent_map, interior_field)


def solution(mesh):
    in_specs = (P("box", None, "row", None), P("box", None, None, None), P("box", "row", None))
    out_specs = (P("box", None, "row", None), P("box", "row", None))
    return jax.shard_map(
        per_device, mesh=mesh, in_specs=in_specs, out_specs=out_specs, check_vma=False
    )
```

time: 99.6 us -> 36.4 us (0.37)
  other arithmetic: 46.7 us -> 0.02 us
  matrix products: 28.1 us -> 0 us
  Pallas kernels: 0 us -> 11.2 us
  local copies, waits for them, and re-layouts: 2.1 us -> 0.01 us
  blocking collectives: 20 us -> 21.8 us
    another operation x7 -> x0, other arithmetic: 44.9 us -> none  [the longest x4 25.1 us: per_device(): factor = jnp.linalg.cholesky(shared_block)]
    dot_general x8 -> x0, matrix products: 26.8 us -> none  [the longest x1 9.88 us: per_device(): jnp.einsum('bro,boq->brq', solution_op[:, :, :outer_size], own_data, pref...]
    pallas_call x0 -> x5, Pallas kernels: none -> 11.2 us  [the longest x2 5.08 us: field(): pl.pallas_call(functools.partial(field_kernel, turn, chunk), out_shape=ou...]
    all_gather x1, blocking collectives: 20 us -> 21.8 us  [per_device(): gathered = lax.all_gather(packed, 'row', axis=0)]
    slice x5 -> x2, local copies, waits for them, and re-layouts: 1.72 us -> 0.01 us  [the longest x1 0.01 us: per_device(): other_rows[:, :, :outer]]
    another operation x1 -> x0, matrix products: 1.23 us -> none  [invert_factor(): lax.linalg.triangular_solve(factor, identity, left_side=True, lower=True)]
    select_n x1 -> x0, other arithmetic: 1.11 us -> none  [per_device(): alpha_edge = jnp.where(is_alpha, own_edge, other_edge)]
    ppermute x2 -> x3, starting transfers between devices: 1.63 us -> 2.48 us  [exchange(): return lax.ppermute(value, axis, pairs)]
  transfers between devices with their start and end apart: 2 -> 3, of which waited for: 0 -> 0; matrix products, arithmetic and copies ran while one was open for 64% -> 0% of each run, Pallas kernels for 0% -> 14%
where the time goes in v3:
time: 36.4 us; the launch traced here: 36.2 us
  blocking collectives  21.8 us (60%)
  Pallas kernels  11.2 us (31%)
  starting transfers between devices  2.48 us (7%)
  between operations  0.71 us (2%)
    all_gather x1, blocking collectives, per_device(): gathered = lax.all_gather(packed, 'row', axis=0)  21.8 us
    pallas_call x2, Pallas kernels, field(): pl.pallas_call(functools.partial(field_kernel, turn, chunk), out_shape=ou...  5.08 us
    pallas_call x1, Pallas kernels, per_device(): pl.pallas_call(functools.partial(early_kernel, chunk), out_shape=(half, p...  2.85 us
    ppermute x3, starting transfers between devices, exchange(): return lax.ppermute(value, axis, pairs)  2.48 us
    pallas_call x1, Pallas kernels, per_device(): pl.pallas_call(solve_kernel, out_shape=jax.ShapeDtypeStruct((edge, loads...  2.18 us
    pallas_call x1, Pallas kernels, per_device(): pl.pallas_call(start_kernel, out_shape=(jax.ShapeDtypeStruct((boxes, loca...  1.13 us
  transfers between devices with their start and end apart: 3, of which 0 were waited for; matrix products, arithmetic and copies ran while one was open for 0% of the time, Pallas kernels for 14%

profile of v3, /device:TPU:1, one launch (start us, length us, event | category | flops | bytes accessed | tf_op | source)
XLA Modules:
  0.0 36.2 jit_solution(6161182647869314275)
XLA Ops:
  0.6 1.1 %start.1 = (f32[2,16,512]{2,1,0:T(8,128)S(1)}, bf16[384,768]{1,0:T(8,128)(2,1)S(1)}) custom-call(s32[1]{0:T(128)} %bitcast.place_ref, f32[2,4,16,512]{3,2,1,0:T(8,128)} %map_ref.3, bf16[2,384,768]{2,1,0:T(8,128)(2,1)} %bitcast.6), custom_call_target="tpu_custom_call" | custom-call | tf_op jit(solution)/shard_map/start/pallas_call | solution.py:221
  1.8 2.1 %collective-permute-start = (f32[2,16,512]{2,1,0:T(8,128)S(1)}, f32[2,16,512]{2,1,0:T(8,128)S(1)}, u32[]{:S(2)}, u32[]{:S(2)}) collective-permute-start(f32[2,16,512]{2,1,0:T(8,128)S(1)} %get-tuple-element.14.rows_ref), channel_id=1, source_target_pairs={{0,8},{8,0},{16,24},{24,16},{32,40},{40,32},{48,56},{56,48},{64,72... | collective-permute-start | bytes 196616 | tf_op jit(solution)/shard_map/ppermute | solution.py:25
  3.9 2.8 %early.1 = (bf16[384,768]{1,0:T(8,128)(2,1)S(1)}, f32[2,3,16,512]{3,2,1,0:T(8,128)S(1)}, bf16[384,768]{1,0:T(8,128)(2,1)S(1)}, bf16[2048,512]{1,0:T(8,128)(2,1)S...) custom-call(s32[1]{0:T(128)} %bitcast.place_ref, ...), custom_call_target="tpu_custom_call", output_to_operand_aliasing={{0}: (1, {})} | custom-call | flops 805306368 | bytes 6291456 | tf_op jit(solution)/shard_map/early/pallas_call | solution.py:232
  6.8 0.1 collective-permute-start.1
  6.9 0.0 collective-permute-done
  6.9 21.8 %all-gather = f32[16,16,896]{2,1,0:T(8,128)S(1)} all-gather(f32[2,16,896]{2,1,0:T(8,128)S(1)} %pad_maximum_fusion), channel_id=2, replica_groups=mesh['box'=32,'row'=8] {'row'}, dimensions={0}, use_global_device_ids=true | all-gather | bytes 1032192 | tf_op jit(solution)/shard_map/all_gather | solution.py:262
  28.7 0.0 collective-permute-done.1.other_ref
  28.7 2.2 %solve.1.solved_ref = bf16[128,1152]{1,0:T(8,128)(2,1)S(1)} custom-call(s32[1]{0:T(128)} %bitcast.place_ref, f32[8,2,16,896]{3,2,1,0:T(8,128)S(1)} %bitcast.3, bf16[384,768]{1,0:T(8,128)(2,1)S(1)} %get-tuple-element.17.own_ref.data_ref, bf16[384,768]{1,0:T(8,128)(2,1)S(1)} %collective-permute-done.1.other_ref), custom_call_target="tpu_custom_call" | custom-call | tf_op jit(solution)/shard_map/solve/pallas_call | solution.py:263
  30.9 0.2 collective-permute-start.2
  31.1 2.2 %field.2 = (bf16[2,2048,768]{2,1,0:T(8,128)(2,1)}, f32[2,3,16,768]{3,2,1,0:T(8,128)}) custom-call(s32[1]{0:T(128)} %bitcast.place_ref, f32[8,2,16,896]{3,2,1,0:T(8,128)S(1)} %bitcast.4, f32[2,3,16,512]{3,2,1,0:T(8,128)S(1)} %get-tuple-element.16.map_ref, bf16[128,1152]{1,0:T(8,128)(2,1)S(1)} %solve.1.solved_ref, ...), custom_call_target="tpu_custom_call" | custom-call | flops 1610612736 | bytes 8388608 | tf_op jit(solution)/shard_map/field/pallas_call | solution.py:279
  33.3 0.0 collective-permute-done.2.solved_ref
  33.3 2.9 %field.3 = (bf16[2,2048,768]{2,1,0:T(8,128)(2,1)}, f32[2,3,16,768]{3,2,1,0:T(8,128)}) custom-call(s32[1]{0:T(128)} %bitcast.place_ref, f32[8,2,16,896]{3,2,1,0:T(8,128)S(1)} %bitcast.5, f32[2,3,16,512]{3,2,1,0:T(8,128)S(1)} %get-tuple-element.16.map_ref, ...), custom_call_target="tpu_custom_call", output_to_operand_aliasing={{0}: (6, {}), {1}: (7, {})} | custom-call | flops 1610612736 | bytes 8388608 | tf_op jit(solution)/shard_map/field/pallas_call | solution.py:279
  (4 shorter events, 0.0 us)
Async XLA Ops:
  1.8 5.1 %collective-permute-start = (f32[2,16,512]{2,1,0:T(8,128)S(1)}, f32[2,16,512]{2,1,0:T(8,128)S(1)}, u32[]{:S(2)}, u32[]{:S(2)}) collective-permute-start(f32[2,16,512]{2,1,0:T(8,128)S(1)} %get-tuple-element.14.rows_ref), channel_id=1, source_target_pairs={{0,8},{8,0},{16,24},{24,16},{32,40},{40,32},{48,56},{56,48},{64,72... | collective-permute-start | bytes 196616 | tf_op jit(solution)/shard_map/ppermute | solution.py:25
  6.8 22.0 %collective-permute-start.1 = (bf16[384,768]{1,0:T(8,128)(2,1)S(1)}, bf16[384,768]{1,0:T(8,128)(2,1)S(1)}, u32[]{:S(2)}, u32[]{:S(2)}) collective-permute-start(bf16[384,768]{1,0:T(8,128)(2,1)S(1)} %get-tuple-element.17.own_ref.data_ref), channel_id=1, source_target_pairs={{0,8},{8,0},{16,24},{24,16},{32,40},{40,32},{48,56},{56,48},{64,72... | collective-permute-start | bytes 1769480 | tf_op jit(solution)/shard_map/ppermute | solution.py:25
  30.9 2.4 %collective-permute-start.2 = (bf16[128,1152]{1,0:T(8,128)(2,1)S(1)}, bf16[128,1152]{1,0:T(8,128)(2,1)S(1)}, u32[]{:S(2)}, u32[]{:S(2)}) collective-permute-start(bf16[128,1152]{1,0:T(8,128)(2,1)S(1)} %solve.1.solved_ref), channel_id=1, source_target_pairs={{0,1},{1,0},{2,3},{3,2},{4,5},{5,4},{6,7},{7,6},{8,9},{9,8},{10,11... | collective-permute-start | bytes 884744 | tf_op jit(solution)/shard_map/ppermute | solution.py:25

commit v4 on v3

v4 whole, which is shorter than its diff:
```python
import functools

import jax
import jax.numpy as jnp
from jax import lax
from jax.experimental import pallas as pl
from jax.experimental.pallas import tpu as pltpu
from jax.sharding import PartitionSpec as P

F32 = jnp.float32
BF16 = jnp.bfloat16
REMAINDER = 2.0**-27
SURE_DOUBLINGS = 4
MOST_DOUBLINGS = 40

SMEM_SPEC = pl.BlockSpec(memory_space=pltpu.SMEM)
VMEM_SPEC = pl.BlockSpec(memory_space=pltpu.VMEM)
HBM_SPEC = pl.BlockSpec(memory_space=pltpu.HBM)
ANY_SPEC = pl.BlockSpec(memory_space=pl.ANY)


def exchange(value, axis):
    pairs = [(source, source ^ 1) for source in range(lax.axis_size(axis))]
    return lax.ppermute(value, axis, pairs)


def in_hbm(value):
    return pltpu.with_memory_space_constraint(value, pltpu.HBM)


def dot(left, right, precision=None):
    return jnp.dot(left, right, precision=precision, preferred_element_type=F32)


def split(value, count):
    pieces = []
    for _ in range(count):
        piece = value.astype(BF16)
        pieces.append(piece)
        value = value - piece.astype(F32)
    return pieces


def split_dot(left, right):
    high, low = split(left, 2)
    right_high, right_low = split(right, 2)
    both = dot(jnp.concatenate([high, low], axis=0), right_high)
    rows = left.shape[0]
    return both[:rows] + (both[rows:] + dot(high, right_low))


def full_dot(left, right):
    return dot(left, right, lax.Precision.HIGHEST)


def start_copies(copies):
    for copy in copies:
        copy.start()


def finish_copies(copies):
    for copy in copies:
        copy.wait()


def start_kernel(place_ref, map_ref, data_ref, rows_ref, first_ref, arrived):
    copies = (
        pltpu.make_async_copy(map_ref.at[:, 3], rows_ref, arrived.at[0]),
        pltpu.make_async_copy(data_ref.at[place_ref[0] & 1], first_ref, arrived.at[1]),
    )
    start_copies(copies)
    finish_copies(copies)


def early_kernel(place_ref, first_ref, rows_ref, operator_ref, sent_ref, near_ref, partial_ref, arrived):
    depth = operator_ref.shape[2] // 2
    copy = pltpu.make_async_copy(operator_ref.at[place_ref[0] & 1], near_ref, arrived.at[0])
    copy.start()
    copy.wait()
    partial_ref[...] = dot(near_ref[:, :depth], first_ref[:depth])


def solve_kernel(
    place_ref,
    gathered_ref,
    own_ref,
    other_ref,
    map_ref,
    data_ref,
    operator_ref,
    solved_ref,
    outer_ref,
    second_ref,
    far_ref,
    sums,
    power_ref,
    arrived,
):
    mine = place_ref[0] & 1
    copies = (
        pltpu.make_async_copy(operator_ref.at[1 - mine], far_ref, arrived.at[0]),
        pltpu.make_async_copy(data_ref.at[1 - mine], second_ref, arrived.at[1]),
        pltpu.make_async_copy(map_ref.at[:, pl.ds(0, 3)], outer_ref, arrived.at[2]),
    )
    start_copies(copies)
    edge = sums.shape[0]
    outer, loads = own_ref.shape
    shared = gathered_ref[:, mine, :, :edge].reshape(edge, edge)
    row = lax.broadcasted_iota(jnp.int32, (edge, edge), 0)
    column = lax.broadcasted_iota(jnp.int32, (edge, edge), 1)
    diagonal = row == column
    kept = jnp.where(diagonal, shared, 0.0)
    scale = 1.0 / jnp.sum(kept, axis=1, keepdims=True)
    right_scale = 1.0 / jnp.sum(kept, axis=0, keepdims=True)
    power = jnp.where(diagonal, 0.0, -shared) * scale
    size = jnp.sum(jnp.abs(power), axis=1, keepdims=True)
    norm = jnp.max(size, axis=0, keepdims=True)[0, 0]

    coupling = gathered_ref[:, mine, :, edge:].reshape(edge, 2 * outer)
    parts = dot(jnp.concatenate(split(coupling[:, :outer], 2), axis=0), own_ref[...])
    parts += dot(jnp.concatenate(split(coupling[:, outer:], 2), axis=0), other_ref[...])
    terms = parts[:edge] + parts[edge:]

    total = jnp.where(diagonal, 1.0, power)
    power = split_dot(power, power)
    for _ in range(SURE_DOUBLINGS - 1):
        both = split_dot(jnp.concatenate([total, power], axis=0), power)
        total = total + both[:edge]
        power = both[edge:]
    sums[...] = total + split_dot(total, power)

    bound = norm
    for _ in range(SURE_DOUBLINGS + 1):
        bound = bound * bound

    @pl.when(bound > REMAINDER)
    def _():
        power_ref[...] = full_dot(power, power)

        def more(carry):
            left, count = carry
            return jnp.logical_and(left > REMAINDER, count < MOST_DOUBLINGS)

        def double(carry):
            left, count = carry
            held = power_ref[...]
            both = full_dot(jnp.concatenate([sums[...], held], axis=0), held)
            sums[...] = sums[...] + both[:edge]
            power_ref[...] = both[edge:]
            return left * left, count + 1

        lax.while_loop(more, double, (bound, jnp.int32(0)))

    inverse = sums[...] * right_scale
    solved_ref[:, :loads] = (-split_dot(inverse, terms)).astype(BF16)
    for order, piece in enumerate(split(inverse, 3)):
        solved_ref[:, loads + order * edge : loads + (order + 1) * edge] = piece
    finish_copies(copies)


def parent_rows(place_ref, gathered_ref, outer_ref, solved_ref, box, loads):
    edge = solved_ref.shape[0]
    outer = 3 * edge
    inverse = jnp.zeros((edge, edge), F32)
    for order in (2, 1, 0):
        inverse = inverse + solved_ref[:, loads + order * edge : loads + (order + 1) * edge].astype(F32)
    rows = outer_ref[box].reshape(-1, 4 * edge)
    weights = split_dot(rows[:, outer:], inverse)
    coupling = gathered_ref[:, box, :, edge:].reshape(edge, 2 * outer)
    change = split_dot(weights, coupling)
    own = rows[:, :outer] - change[:, :outer]
    other = -change[:, outer:]
    is_alpha = place_ref[0] < 2
    left = jnp.where(is_alpha, own, other)
    right = jnp.where(is_alpha, other, own)
    return jnp.concatenate([left, right], axis=1).reshape(3, -1, 2 * outer)


def middle_kernel(
    place_ref, gathered_ref, outer_ref, solved_ref, second_ref, far_ref, partial_ref, parent_ref
):
    depth = far_ref.shape[1] // 2
    loads = second_ref.shape[1]
    partial_ref[...] = dot(far_ref[:, :depth], second_ref[:depth])
    parent_ref[...] = parent_rows(
        place_ref, gathered_ref, outer_ref, solved_ref, place_ref[0] & 1, loads
    )


def field_kernel(
    chunk,
    place_ref,
    gathered_ref,
    outer_ref,
    solved_ref,
    swapped_ref,
    first_ref,
    second_ref,
    near_ref,
    far_ref,
    near_part_ref,
    far_part_ref,
    ready_ref,
    field_ref,
    parent_ref,
    pressure,
    finished,
    parent,
    left,
):
    mine = place_ref[0] & 1
    outer, loads = first_ref.shape
    cells, points = near_ref.shape
    depth = points // 2
    cuts = [slice(start, start + chunk) for start in range(0, cells, chunk)]
    copy = pltpu.make_async_copy(ready_ref, parent_ref.at[mine], left.at[0])
    copy.start()
    writes = [copy]
    turns = (
        (mine, solved_ref, first_ref, near_ref, near_part_ref),
        (1 - mine, swapped_ref, second_ref, far_ref, far_part_ref),
    )
    for turn, (box, edge_ref, data_ref, operator_ref, part_ref) in enumerate(turns):
        pressure[turn, : outer - depth] = data_ref[depth:]
        pressure[turn, outer - depth :] = edge_ref[:, :loads]
        for cut in cuts:
            total = part_ref[cut] + dot(operator_ref[cut, depth:], pressure[turn])
            finished[turn, cut] = total.astype(BF16)
            copy = pltpu.make_async_copy(
                finished.at[turn, cut], field_ref.at[box, cut], left.at[len(writes)]
            )
            copy.start()
            writes.append(copy)
    parent[...] = parent_rows(place_ref, gathered_ref, outer_ref, swapped_ref, 1 - mine, loads)
    copy = pltpu.make_async_copy(parent, parent_ref.at[1 - mine], left.at[len(writes)])
    copy.start()
    writes.append(copy)
    finish_copies(writes)


def per_device(dtn_map, boundary_data, solution_op):
    boxes, _, local, points = dtn_map.shape
    edge = boundary_data.shape[2]
    loads = boundary_data.shape[3]
    cells = solution_op.shape[1]
    outer = 3 * edge
    side = lax.axis_index("box") & 1
    core = lax.axis_index("row") & 1
    place = (2 * side + core).astype(jnp.int32).reshape(1)
    whole_map = in_hbm(dtn_map)
    data = in_hbm(boundary_data.reshape(boxes, outer, loads))
    operator = in_hbm(solution_op)
    half = jax.ShapeDtypeStruct((outer, loads), BF16)
    part = pltpu.VMEM((cells, loads), F32)
    own_rows, first = pl.pallas_call(
        start_kernel,
        out_shape=(jax.ShapeDtypeStruct((boxes, local, points), F32), half),
        in_specs=[SMEM_SPEC, HBM_SPEC, HBM_SPEC],
        out_specs=(VMEM_SPEC, VMEM_SPEC),
        scratch_shapes=[pltpu.SemaphoreType.DMA((2,))],
        compiler_params=pltpu.CompilerParams(vmem_limit_bytes=4 << 20),
        name="start",
    )(place, whole_map, data)
    other_rows = exchange(own_rows, "box")
    first, near, near_part = pl.pallas_call(
        early_kernel,
        out_shape=(half, pltpu.VMEM((cells, points), BF16), part),
        in_specs=[SMEM_SPEC, VMEM_SPEC, ANY_SPEC, HBM_SPEC],
        out_specs=(VMEM_SPEC,) * 3,
        scratch_shapes=[pltpu.SemaphoreType.DMA((1,))],
        input_output_aliases={1: 0},
        compiler_params=pltpu.CompilerParams(vmem_limit_bytes=4 << 20),
        cost_estimate=pl.CostEstimate(
            flops=cells * points * loads, bytes_accessed=6 << 20, transcendentals=0
        ),
        name="early",
    )(place, first, own_rows, operator)
    crossed = exchange(first, "box")
    packed = jnp.concatenate(
        [
            own_rows[:, :, outer:] + other_rows[:, :, outer:],
            own_rows[:, :, :outer],
            other_rows[:, :, :outer],
        ],
        axis=2,
    )
    gathered = lax.all_gather(packed, "row", axis=0)
    solved, outer_rows, second, far = pl.pallas_call(
        solve_kernel,
        out_shape=(
            jax.ShapeDtypeStruct((edge, loads + 3 * edge), BF16),
            pltpu.VMEM((boxes, 3, local, points), F32),
            pltpu.VMEM((outer, loads), BF16),
            pltpu.VMEM((cells, points), BF16),
        ),
        in_specs=[SMEM_SPEC] + [VMEM_SPEC] * 3 + [HBM_SPEC] * 3,
        out_specs=(VMEM_SPEC,) * 4,
        scratch_shapes=[
            pltpu.VMEM((edge, edge), F32),
            pltpu.VMEM((edge, edge), F32),
            pltpu.SemaphoreType.DMA((3,)),
        ],
        compiler_params=pltpu.CompilerParams(vmem_limit_bytes=12 << 20),
        name="solve",
    )(place, gathered, first, crossed, whole_map, data, operator)
    swapped = exchange(solved, "row")
    far_part, ready = pl.pallas_call(
        middle_kernel,
        out_shape=(part, pltpu.VMEM((3, local, 2 * outer), F32)),
        in_specs=[SMEM_SPEC] + [VMEM_SPEC] * 5,
        out_specs=(VMEM_SPEC,) * 2,
        compiler_params=pltpu.CompilerParams(vmem_limit_bytes=6 << 20),
        cost_estimate=pl.CostEstimate(
            flops=cells * points * loads, bytes_accessed=6 << 20, transcendentals=0
        ),
        name="middle",
    )(place, gathered, outer_rows, solved, second, far)
    chunk = 256
    interior_field, parent_map = pl.pallas_call(
        functools.partial(field_kernel, chunk),
        out_shape=(
            jax.ShapeDtypeStruct((boxes, cells, loads), BF16),
            jax.ShapeDtypeStruct((boxes, 3, local, 2 * outer), F32),
        ),
        in_specs=[SMEM_SPEC] + [VMEM_SPEC] * 11,
        out_specs=(ANY_SPEC, ANY_SPEC),
        scratch_shapes=[
            pltpu.VMEM((boxes, points - points // 2, loads), BF16),
            pltpu.VMEM((boxes, cells, loads), BF16),
            pltpu.VMEM((3, local, 2 * outer), F32),
            pltpu.SemaphoreType.DMA((boxes * cells // chunk + 2,)),
        ],
        compiler_params=pltpu.CompilerParams(vmem_limit_bytes=16 << 20),
        name="field",
    )(
        place,
        gathered,
        outer_rows,
        solved,
        swapped,
        first,
        second,
        near,
        far,
        near_part,
        far_part,
        ready,
    )
    return (parent_map, interior_field)


def solution(mesh):
    in_specs = (P("box", None, "row", None), P("box", None, None, None), P("box", "row", None))
    out_specs = (P("box", None, "row", None), P("box", "row", None))
    return jax.shard_map(
        per_device, mesh=mesh, in_specs=in_specs, out_specs=out_specs, check_vma=False
    )
```

time: 36.4 us -> 35.5 us (0.975)
  Pallas kernels: 11.2 us -> 10.1 us
    pallas_call x4, Pallas kernels: 10.1 us -> 9.02 us  [the longest x1 3.13 us: per_device(): pl.pallas_call(functools.partial(field_kernel, chunk), out_shape=(jax.Sha...]
  transfers between devices with their start and end apart: 3 -> 3, of which waited for: 0 -> 1; matrix products, arithmetic and copies ran while one was open for 0% -> 0% of each run, Pallas kernels for 14% -> 11%
where the time goes in v4:
time: 35.5 us; the launch traced here: 35.3 us
  blocking collectives  21.7 us (61%)
  Pallas kernels  10.1 us (28%)
  starting transfers between devices  2.47 us (7%)
  between operations  0.71 us (2%)
    all_gather x1, blocking collectives, per_device(): gathered = lax.all_gather(packed, 'row', axis=0)  21.7 us
    pallas_call x1, Pallas kernels, per_device(): pl.pallas_call(functools.partial(field_kernel, chunk), out_shape=(jax.Sha...  3.13 us
    pallas_call x1, Pallas kernels, per_device(): pl.pallas_call(early_kernel, out_shape=(half, pltpu.VMEM((cells, points),...  2.58 us
    ppermute x3, starting transfers between devices, exchange(): return lax.ppermute(value, axis, pairs)  2.47 us
    pallas_call x1, Pallas kernels, per_device(): pl.pallas_call(solve_kernel, out_shape=(jax.ShapeDtypeStruct((edge, loads...  2.14 us
    pallas_call x1, Pallas kernels, per_device(): pl.pallas_call(middle_kernel, out_shape=(part, pltpu.VMEM((3, local, 2 *...  1.16 us
    pallas_call x1, Pallas kernels, per_device(): pl.pallas_call(start_kernel, out_shape=(jax.ShapeDtypeStruct((boxes, loca...  1.13 us
  transfers between devices with their start and end apart: 3, of which 1 were waited for; matrix products, arithmetic and copies ran while one was open for 0% of the time, Pallas kernels for 11%

profile of v4, /device:TPU:1, one launch (start us, length us, event | category | flops | bytes accessed | tf_op | source)
XLA Modules:
  0.0 35.3 jit_solution(3781667512866410854)
XLA Ops:
  0.6 1.1 %start.1 = (f32[2,16,512]{2,1,0:T(8,128)S(1)}, bf16[384,768]{1,0:T(8,128)(2,1)S(1)}) custom-call(s32[1]{0:T(128)} %bitcast.place_ref, f32[2,4,16,512]{3,2,1,0:T(8,128)} %map_ref.3, bf16[2,384,768]{2,1,0:T(8,128)(2,1)} %bitcast.6), custom_call_target="tpu_custom_call" | custom-call | tf_op jit(solution)/shard_map/start/pallas_call | solution.py:255
  1.8 2.1 %collective-permute-start = (f32[2,16,512]{2,1,0:T(8,128)S(1)}, f32[2,16,512]{2,1,0:T(8,128)S(1)}, u32[]{:S(2)}, u32[]{:S(2)}) collective-permute-start(f32[2,16,512]{2,1,0:T(8,128)S(1)} %get-tuple-element.15.rows_ref), channel_id=1, source_target_pairs={{0,8},{8,0},{16,24},{24,16},{32,40},{40,32},{48,56},{56,48},{64,72... | collective-permute-start | bytes 196616 | tf_op jit(solution)/shard_map/ppermute | solution.py:24
  3.9 2.6 %early.1 = (bf16[384,768]{1,0:T(8,128)(2,1)S(1)}, bf16[2048,512]{1,0:T(8,128)(2,1)S(1)}, f32[2048,768]{1,0:T(8,128)S(1)}) custom-call(s32[1]{0:T(128)} %bitcast.place_ref, bf16[384,768]{1,0:T(8,128)(2,1)S(1)} %get-tuple-element.16.first_ref, f32[2,16,512]{2,1,0:T(8,128)S(1)} %get-tuple-element.15.rows_ref, ...), custom_call_target="tpu_custom_call", output_to_operand_aliasing={{0}: (1, {})} | custom-call | flops 805306368 | bytes 6291456 | tf_op jit(solution)/shard_map/early/pallas_call | solution.py:265
  6.5 0.1 collective-permute-start.1
  6.6 0.0 collective-permute-done
  6.7 21.7 %all-gather = f32[16,16,896]{2,1,0:T(8,128)S(1)} all-gather(f32[2,16,896]{2,1,0:T(8,128)S(1)} %pad_maximum_fusion), channel_id=2, replica_groups=mesh['box'=32,'row'=8] {'row'}, dimensions={0}, use_global_device_ids=true | all-gather | bytes 1032192 | tf_op jit(solution)/shard_map/all_gather | solution.py:287
  28.4 0.0 collective-permute-done.1.other_ref
  28.4 2.1 %solve.1 = (bf16[128,1152]{1,0:T(8,128)(2,1)S(1)}, f32[2,3,16,512]{3,2,1,0:T(8,128)S(1)}, bf16[384,768]{1,0:T(8,128)(2,1)S(1)}, bf16[2048,512]{1,0:T(8,128)(2,1)S(1)}) custom-call(s32[1]{0:T(128)} %bitcast.place_ref, f32[8,2,16,896]{3,2,1,0:T(8,128)S(1)} %bitcast.3, bf16[384,768]{1,0:T(8,128)(2,1)S(1)} %get-tuple-element.17.own_ref.first_ref, ...), custom_call_target="tpu_custom_call" | custom-call | tf_op jit(solution)/shard_map/solve/pallas_call | solution.py:288
  30.5 0.2 collective-permute-start.2
  30.8 1.2 %middle.1 = (f32[2048,768]{1,0:T(8,128)S(1)}, f32[3,16,768]{2,1,0:T(8,128)S(1)}) custom-call(s32[1]{0:T(128)} %bitcast.place_ref, f32[8,2,16,896]{3,2,1,0:T(8,128)S(1)} %bitcast.4, f32[2,3,16,512]{3,2,1,0:T(8,128)S(1)} %get-tuple-element.18.outer_ref, bf16[128,1152]{1,0:T(8,128)(2,1)S(1)} %get-tuple-element.19.solved_ref, ...), custom_call_target="tpu_custom_call" | custom-call | flops 805306368 | bytes 6291456 | tf_op jit(solution)/shard_map/middle/pallas_call | solution.py:307
  31.9 0.3 collective-permute-done.2.swapped_ref
  32.2 3.1 %field.1 = (bf16[2,2048,768]{2,1,0:T(8,128)(2,1)}, f32[2,3,16,768]{3,2,1,0:T(8,128)}) custom-call(s32[1]{0:T(128)} %bitcast.place_ref, f32[8,2,16,896]{3,2,1,0:T(8,128)S(1)} %bitcast.5, f32[2,3,16,512]{3,2,1,0:T(8,128)S(1)} %get-tuple-element.18.outer_ref, bf16[128,1152]{1,0:T(8,128)(2,1)S(1)} %get-tuple-element.19.solved_ref, ...), custom_call_target="tpu_custom_call" | custom-call | tf_op jit(solution)/shard_map/field/pallas_call | solution.py:319
  (4 shorter events, 0.0 us)
Async XLA Ops:
  1.8 4.8 %collective-permute-start = (f32[2,16,512]{2,1,0:T(8,128)S(1)}, f32[2,16,512]{2,1,0:T(8,128)S(1)}, u32[]{:S(2)}, u32[]{:S(2)}) collective-permute-start(f32[2,16,512]{2,1,0:T(8,128)S(1)} %get-tuple-element.15.rows_ref), channel_id=1, source_target_pairs={{0,8},{8,0},{16,24},{24,16},{32,40},{40,32},{48,56},{56,48},{64,72... | collective-permute-start | bytes 196616 | tf_op jit(solution)/shard_map/ppermute | solution.py:24
  6.5 21.9 %collective-permute-start.1 = (bf16[384,768]{1,0:T(8,128)(2,1)S(1)}, bf16[384,768]{1,0:T(8,128)(2,1)S(1)}, u32[]{:S(2)}, u32[]{:S(2)}) collective-permute-start(bf16[384,768]{1,0:T(8,128)(2,1)S(1)} %get-tuple-element.17.own_ref.first_ref), channel_id=1, source_target_pairs={{0,8},{8,0},{16,24},{24,16},{32,40},{40,32},{48,56},{56,48},{64,72... | collective-permute-start | bytes 1769480 | tf_op jit(solution)/shard_map/ppermute | solution.py:24
  30.5 1.7 %collective-permute-start.2 = (bf16[128,1152]{1,0:T(8,128)(2,1)S(1)}, bf16[128,1152]{1,0:T(8,128)(2,1)S(1)}, u32[]{:S(2)}, u32[]{:S(2)}) collective-permute-start(bf16[128,1152]{1,0:T(8,128)(2,1)S(1)} %get-tuple-element.19.solved_ref), channel_id=1, source_target_pairs={{0,1},{1,0},{2,3},{3,2},{4,5},{5,4},{6,7},{7,6},{8,9},{9,8},{10,11... | collective-permute-start | bytes 884744 | tf_op jit(solution)/shard_map/ppermute | solution.py:24

commit v5 on v4

--- a/solution.py
+++ b/solution.py
@@ -72,12 +72,35 @@
     finish_copies(copies)
 
 
-def early_kernel(place_ref, first_ref, rows_ref, operator_ref, sent_ref, near_ref, partial_ref, arrived):
+def order_kernel(first_ref, rows_ref, same_ref):
+    pass
+
+
+def early_kernel(
+    place_ref,
+    first_ref,
+    map_ref,
+    data_ref,
+    operator_ref,
+    near_ref,
+    partial_ref,
+    outer_ref,
+    second_ref,
+    far_ref,
+    arrived,
+):
+    mine = place_ref[0] & 1
     depth = operator_ref.shape[2] // 2
-    copy = pltpu.make_async_copy(operator_ref.at[place_ref[0] & 1], near_ref, arrived.at[0])
-    copy.start()
-    copy.wait()
+    copies = (
+        pltpu.make_async_copy(operator_ref.at[mine], near_ref, arrived.at[0]),
+        pltpu.make_async_copy(operator_ref.at[1 - mine], far_ref, arrived.at[1]),
+        pltpu.make_async_copy(data_ref.at[1 - mine], second_ref, arrived.at[2]),
+        pltpu.make_async_copy(map_ref.at[:, pl.ds(0, 3)], outer_ref, arrived.at[3]),
+    )
+    start_copies(copies)
+    copies[0].wait()
     partial_ref[...] = dot(near_ref[:, :depth], first_ref[:depth])
+    finish_copies(copies[1:])
 
 
 def solve_kernel(
@@ -85,24 +108,12 @@
     gathered_ref,
     own_ref,
     other_ref,
-    map_ref,
-    data_ref,
-    operator_ref,
     solved_ref,
-    outer_ref,
-    second_ref,
-    far_ref,
     sums,
     power_ref,
-    arrived,
+    terms_ref,
 ):
     mine = place_ref[0] & 1
-    copies = (
-        pltpu.make_async_copy(operator_ref.at[1 - mine], far_ref, arrived.at[0]),
-        pltpu.make_async_copy(data_ref.at[1 - mine], second_ref, arrived.at[1]),
-        pltpu.make_async_copy(map_ref.at[:, pl.ds(0, 3)], outer_ref, arrived.at[2]),
-    )
-    start_copies(copies)
     edge = sums.shape[0]
     outer, loads = own_ref.shape
     shared = gathered_ref[:, mine, :, :edge].reshape(edge, edge)
@@ -127,15 +138,26 @@
         both = split_dot(jnp.concatenate([total, power], axis=0), power)
         total = total + both[:edge]
         power = both[edge:]
-    sums[...] = total + split_dot(total, power)
-
+    total = total + split_dot(total, power)
+    sums[...] = total
+    power_ref[...] = power
+    terms_ref[...] = terms
+
+    def hand_out(total, terms):
+        inverse = total * right_scale
+        solved_ref[:, :loads] = (-split_dot(inverse, terms)).astype(BF16)
+        for order, piece in enumerate(split(inverse, 3)):
+            solved_ref[:, loads + order * edge : loads + (order + 1) * edge] = piece
+
+    hand_out(total, terms)
     bound = norm
     for _ in range(SURE_DOUBLINGS + 1):
         bound = bound * bound
 
     @pl.when(bound > REMAINDER)
     def _():
-        power_ref[...] = full_dot(power, power)
+        last = power_ref[...]
+        power_ref[...] = full_dot(last, last)
 
         def more(carry):
             left, count = carry
@@ -150,12 +172,7 @@
             return left * left, count + 1
 
         lax.while_loop(more, double, (bound, jnp.int32(0)))
-
-    inverse = sums[...] * right_scale
-    solved_ref[:, :loads] = (-split_dot(inverse, terms)).astype(BF16)
-    for order, piece in enumerate(split(inverse, 3)):
-        solved_ref[:, loads + order * edge : loads + (order + 1) * edge] = piece
-    finish_copies(copies)
+        hand_out(sums[...], terms_ref[...])
 
 
 def parent_rows(place_ref, gathered_ref, outer_ref, solved_ref, box, loads):
@@ -262,20 +279,35 @@
         name="start",
     )(place, whole_map, data)
     other_rows = exchange(own_rows, "box")
-    first, near, near_part = pl.pallas_call(
+    first = pl.pallas_call(
+        order_kernel,
+        out_shape=half,
+        in_specs=[ANY_SPEC, ANY_SPEC],
+        out_specs=ANY_SPEC,
+        input_output_aliases={0: 0},
+        compiler_params=pltpu.CompilerParams(vmem_limit_bytes=1 << 20),
+        name="order",
+    )(first, own_rows)
+    crossed = exchange(first, "box")
+    near, near_part, outer_rows, second, far = pl.pallas_call(
         early_kernel,
-        out_shape=(half, pltpu.VMEM((cells, points), BF16), part),
-        in_specs=[SMEM_SPEC, VMEM_SPEC, ANY_SPEC, HBM_SPEC],
-        out_specs=(VMEM_SPEC,) * 3,
-        scratch_shapes=[pltpu.SemaphoreType.DMA((1,))],
-        input_output_aliases={1: 0},
+        out_shape=(
+            pltpu.VMEM((cells, points), BF16),
+            part,
+            pltpu.VMEM((boxes, 3, local, points), F32),
+            pltpu.VMEM((outer, loads), BF16),
+            pltpu.VMEM((cells, points), BF16),
+        ),
+        in_specs=[SMEM_SPEC, VMEM_SPEC, HBM_SPEC, HBM_SPEC, HBM_SPEC],
+        out_specs=(VMEM_SPEC,) * 5,
+        scratch_shapes=[pltpu.SemaphoreType.DMA((4,))],
         compiler_params=pltpu.CompilerParams(vmem_limit_bytes=4 << 20),
         cost_estimate=pl.CostEstimate(
             flops=cells * points * loads, bytes_accessed=6 << 20, transcendentals=0
         ),
         name="early",
-    )(place, first, own_rows, operator)
-    crossed = exchange(first, "box")
+    )(place, first, whole_map, data, operator)
+    other_rows, near = lax.optimization_barrier((other_rows, near))
     packed = jnp.concatenate(
         [
             own_rows[:, :, outer:] + other_rows[:, :, outer:],
@@ -285,24 +317,19 @@
         axis=2,
     )
     gathered = lax.all_gather(packed, "row", axis=0)
-    solved, outer_rows, second, far = pl.pallas_call(
+    solved = pl.pallas_call(
         solve_kernel,
-        out_shape=(
-            jax.ShapeDtypeStruct((edge, loads + 3 * edge), BF16),
-            pltpu.VMEM((boxes, 3, local, points), F32),
-            pltpu.VMEM((outer, loads), BF16),
-            pltpu.VMEM((cells, points), BF16),
-        ),
-        in_specs=[SMEM_SPEC] + [VMEM_SPEC] * 3 + [HBM_SPEC] * 3,
-        out_specs=(VMEM_SPEC,) * 4,
+        out_shape=jax.ShapeDtypeStruct((edge, loads + 3 * edge), BF16),
+        in_specs=[SMEM_SPEC] + [VMEM_SPEC] * 3,
+        out_specs=VMEM_SPEC,
         scratch_shapes=[
             pltpu.VMEM((edge, edge), F32),
             pltpu.VMEM((edge, edge), F32),
-            pltpu.SemaphoreType.DMA((3,)),
+            pltpu.VMEM((edge, loads), F32),
         ],
         compiler_params=pltpu.CompilerParams(vmem_limit_bytes=12 << 20),
         name="solve",
-    )(place, gathered, first, crossed, whole_map, data, operator)
+    )(place, gathered, first, crossed)
     swapped = exchange(solved, "row")
     far_part, ready = pl.pallas_call(
         middle_kernel,

time: 35.5 us -> 35.1 us (0.989)
  Pallas kernels: 10.1 us -> 9.72 us
    pallas_call x2 -> x3, Pallas kernels: 4.73 us -> 4.3 us  [the longest x1 2.61 us: per_device(): pl.pallas_call(early_kernel, out_shape=(pltpu.VMEM((cells, points), BF16)...]
where the time goes in v5:
time: 35.1 us; the launch traced here: 35 us
  blocking collectives  21.8 us (62%)
  Pallas kernels  9.72 us (28%)
  starting transfers between devices  2.48 us (7%)
  between operations  0.7 us (2%)
    all_gather x1, blocking collectives, per_device(): gathered = lax.all_gather(packed, 'row', axis=0)  21.8 us
    pallas_call x1, Pallas kernels, per_device(): pl.pallas_call(functools.partial(field_kernel, chunk), out_shape=(jax.Sha...  3.13 us
    pallas_call x1, Pallas kernels, per_device(): pl.pallas_call(early_kernel, out_shape=(pltpu.VMEM((cells, points), BF16)...  2.61 us
    ppermute x3, starting transfers between devices, exchange(): return lax.ppermute(value, axis, pairs)  2.48 us
    pallas_call x1, Pallas kernels, per_device(): pl.pallas_call(solve_kernel, out_shape=jax.ShapeDtypeStruct((edge, loads...  1.69 us
    pallas_call x1, Pallas kernels, per_device(): pl.pallas_call(middle_kernel, out_shape=(part, pltpu.VMEM((3, local, 2 *...  1.16 us
    pallas_call x1, Pallas kernels, per_device(): pl.pallas_call(start_kernel, out_shape=(jax.ShapeDtypeStruct((boxes, loca...  1.13 us
  transfers between devices with their start and end apart: 3, of which 1 were waited for; matrix products, arithmetic and copies ran while one was open for 0% of the time, Pallas kernels for 11%

profile of v5, /device:TPU:1, one launch (start us, length us, event | category | flops | bytes accessed | tf_op | source)
XLA Modules:
  0.0 35.0 jit_solution(16509236765604743339)
XLA Ops:
  0.6 1.1 %start.1 = (f32[2,16,512]{2,1,0:T(8,128)S(1)}, bf16[384,768]{1,0:T(8,128)(2,1)S(1)}) custom-call(s32[1]{0:T(128)} %bitcast.place_ref, f32[2,4,16,512]{3,2,1,0:T(8,128)} %map_ref.3, bf16[2,384,768]{2,1,0:T(8,128)(2,1)} %bitcast.6), custom_call_target="tpu_custom_call" | custom-call | tf_op jit(solution)/shard_map/start/pallas_call | solution.py:272
  1.8 2.1 %collective-permute-start = (f32[2,16,512]{2,1,0:T(8,128)S(1)}, f32[2,16,512]{2,1,0:T(8,128)S(1)}, u32[]{:S(2)}, u32[]{:S(2)}) collective-permute-start(f32[2,16,512]{2,1,0:T(8,128)S(1)} %get-tuple-element.15.rows_ref), channel_id=1, source_target_pairs={{0,8},{8,0},{16,24},{24,16},{32,40},{40,32},{48,56},{56,48},{64,72... | collective-permute-start | bytes 196616 | tf_op jit(solution)/shard_map/ppermute | solution.py:24
  3.9 0.1 collective-permute-start.1
  4.0 2.6 %early.1 = (bf16[2048,512]{1,0:T(8,128)(2,1)S(1)}, f32[2048,768]{1,0:T(8,128)S(1)}, f32[2,3,16,512]{3,2,1,0:T(8,128)S(1)}, bf16[384,768]{1,0:T(8,128)(2,1)S(1)}, bf16[2048,512]{1,0:T(8,128)(2,1)S(1)}) custom-call(s32[1]{0:T(128)} %bitcast.place_ref, bf16[384,768]{1,0:T(8,128)(2,1)S(1)} %order.1.first_ref.own_ref, f32[2,4,16,512]{3,2,1,0:T(8,128)} %map_ref.3, ...), custom_call_target="tpu_custom_call" | custom-call | flops 805306368 | bytes 6291456 | tf_op jit(solution)/shard_map/early/pallas_call | solution.py:292
  6.6 0.0 collective-permute-done
  6.7 21.8 %all-gather = f32[16,16,896]{2,1,0:T(8,128)S(1)} all-gather(f32[2,16,896]{2,1,0:T(8,128)S(1)} %pad_maximum_fusion), channel_id=2, replica_groups=mesh['box'=32,'row'=8] {'row'}, dimensions={0}, use_global_device_ids=true | all-gather | bytes 1032192 | tf_op jit(solution)/shard_map/all_gather | solution.py:319
  28.5 0.0 collective-permute-done.1.other_ref
  28.5 1.7 %solve.1.solved_ref = bf16[128,1152]{1,0:T(8,128)(2,1)S(1)} custom-call(s32[1]{0:T(128)} %bitcast.place_ref, f32[8,2,16,896]{3,2,1,0:T(8,128)S(1)} %bitcast.3, bf16[384,768]{1,0:T(8,128)(2,1)S(1)} %order.1.first_ref.own_ref, bf16[384,768]{1,0:T(8,128)(2,1)S(1)} %collective-permute-done.1.other_ref), custom_call_target="tpu_custom_call" | custom-call | tf_op jit(solution)/shard_map/solve/pallas_call | solution.py:320
  30.2 0.2 collective-permute-start.2
  30.4 1.2 %middle.1 = (f32[2048,768]{1,0:T(8,128)S(1)}, f32[3,16,768]{2,1,0:T(8,128)S(1)}) custom-call(s32[1]{0:T(128)} %bitcast.place_ref, f32[8,2,16,896]{3,2,1,0:T(8,128)S(1)} %bitcast.4, f32[2,3,16,512]{3,2,1,0:T(8,128)S(1)} %get-tuple-element.19.outer_ref, bf16[128,1152]{1,0:T(8,128)(2,1)S(1)} %solve.1.solved_ref, ...), custom_call_target="tpu_custom_call" | custom-call | flops 805306368 | bytes 6291456 | tf_op jit(solution)/shard_map/middle/pallas_call | solution.py:334
  31.6 0.3 collective-permute-done.2.swapped_ref
  31.8 3.1 %field.1 = (bf16[2,2048,768]{2,1,0:T(8,128)(2,1)}, f32[2,3,16,768]{3,2,1,0:T(8,128)}) custom-call(s32[1]{0:T(128)} %bitcast.place_ref, f32[8,2,16,896]{3,2,1,0:T(8,128)S(1)} %bitcast.5, f32[2,3,16,512]{3,2,1,0:T(8,128)S(1)} %get-tuple-element.19.outer_ref, bf16[128,1152]{1,0:T(8,128)(2,1)S(1)} %solve.1.solved_ref, ...), custom_call_target="tpu_custom_call" | custom-call | tf_op jit(solution)/shard_map/field/pallas_call | solution.py:346
  (5 shorter events, 0.0 us)
Async XLA Ops:
  1.8 4.9 %collective-permute-start = (f32[2,16,512]{2,1,0:T(8,128)S(1)}, f32[2,16,512]{2,1,0:T(8,128)S(1)}, u32[]{:S(2)}, u32[]{:S(2)}) collective-permute-start(f32[2,16,512]{2,1,0:T(8,128)S(1)} %get-tuple-element.15.rows_ref), channel_id=1, source_target_pairs={{0,8},{8,0},{16,24},{24,16},{32,40},{40,32},{48,56},{56,48},{64,72... | collective-permute-start | bytes 196616 | tf_op jit(solution)/shard_map/ppermute | solution.py:24
  3.9 24.6 %collective-permute-start.1 = (bf16[384,768]{1,0:T(8,128)(2,1)S(1)}, bf16[384,768]{1,0:T(8,128)(2,1)S(1)}, u32[]{:S(2)}, u32[]{:S(2)}) collective-permute-start(bf16[384,768]{1,0:T(8,128)(2,1)S(1)} %order.1.first_ref.own_ref), channel_id=1, source_target_pairs={{0,8},{8,0},{16,24},{24,16},{32,40},{40,32},{48,56},{56,48},{64,72... | collective-permute-start | bytes 1769480 | tf_op jit(solution)/shard_map/ppermute | solution.py:24
  30.2 1.7 %collective-permute-start.2 = (bf16[128,1152]{1,0:T(8,128)(2,1)S(1)}, bf16[128,1152]{1,0:T(8,128)(2,1)S(1)}, u32[]{:S(2)}, u32[]{:S(2)}) collective-permute-start(bf16[128,1152]{1,0:T(8,128)(2,1)S(1)} %solve.1.solved_ref), channel_id=1, source_target_pairs={{0,1},{1,0},{2,3},{3,2},{4,5},{5,4},{6,7},{7,6},{8,9},{9,8},{10,11... | collective-permute-start | bytes 884744 | tf_op jit(solution)/shard_map/ppermute | solution.py:24

commit v6 on v5

--- a/solution.py
+++ b/solution.py
@@ -1,5 +1,3 @@
-import functools
-
 import jax
 import jax.numpy as jnp
 from jax import lax
@@ -63,25 +61,19 @@
         copy.wait()
 
 
-def start_kernel(place_ref, map_ref, data_ref, rows_ref, first_ref, arrived):
-    copies = (
-        pltpu.make_async_copy(map_ref.at[:, 3], rows_ref, arrived.at[0]),
-        pltpu.make_async_copy(data_ref.at[place_ref[0] & 1], first_ref, arrived.at[1]),
-    )
-    start_copies(copies)
-    finish_copies(copies)
-
-
-def order_kernel(first_ref, rows_ref, same_ref):
-    pass
+def start_kernel(map_ref, rows_ref, arrived):
+    copy = pltpu.make_async_copy(map_ref.at[:, 3], rows_ref, arrived.at[0])
+    copy.start()
+    copy.wait()
 
 
 def early_kernel(
     place_ref,
-    first_ref,
+    rows_ref,
     map_ref,
     data_ref,
     operator_ref,
+    first_ref,
     near_ref,
     partial_ref,
     outer_ref,
@@ -92,15 +84,16 @@
     mine = place_ref[0] & 1
     depth = operator_ref.shape[2] // 2
     copies = (
-        pltpu.make_async_copy(operator_ref.at[mine], near_ref, arrived.at[0]),
-        pltpu.make_async_copy(operator_ref.at[1 - mine], far_ref, arrived.at[1]),
-        pltpu.make_async_copy(data_ref.at[1 - mine], second_ref, arrived.at[2]),
-        pltpu.make_async_copy(map_ref.at[:, pl.ds(0, 3)], outer_ref, arrived.at[3]),
+        pltpu.make_async_copy(data_ref.at[mine], first_ref, arrived.at[0]),
+        pltpu.make_async_copy(operator_ref.at[mine], near_ref, arrived.at[1]),
+        pltpu.make_async_copy(operator_ref.at[1 - mine], far_ref, arrived.at[2]),
+        pltpu.make_async_copy(data_ref.at[1 - mine], second_ref, arrived.at[3]),
+        pltpu.make_async_copy(map_ref.at[:, pl.ds(0, 3)], outer_ref, arrived.at[4]),
     )
     start_copies(copies)
-    copies[0].wait()
+    finish_copies(copies[:2])
     partial_ref[...] = dot(near_ref[:, :depth], first_ref[:depth])
-    finish_copies(copies[1:])
+    finish_copies(copies[2:])
 
 
 def solve_kernel(
@@ -193,31 +186,44 @@
     return jnp.concatenate([left, right], axis=1).reshape(3, -1, 2 * outer)
 
 
+def finish_field(box, edge_ref, data_ref, operator_ref, part_ref, field_ref, pressure, finished, left):
+    outer = data_ref.shape[0]
+    cells, points = operator_ref.shape
+    depth = points // 2
+    loads = data_ref.shape[1]
+    pieces = left.shape[0] - 1
+    chunk = cells // pieces
+    pressure[: outer - depth] = data_ref[depth:]
+    pressure[outer - depth :] = edge_ref[:, :loads]
+    writes = []
+    for order in range(pieces):
+        cut = slice(order * chunk, (order + 1) * chunk)
+        total = part_ref[cut] + dot(operator_ref[cut, depth:], pressure[...])
+        finished[cut] = total.astype(BF16)
+        copy = pltpu.make_async_copy(finished.at[cut], field_ref.at[box, cut], left.at[order])
+        copy.start()
+        writes.append(copy)
+    return writes
+
+
+def finish_parent(place_ref, gathered_ref, outer_ref, edge_ref, box, loads, parent_ref, parent, left):
+    parent[...] = parent_rows(place_ref, gathered_ref, outer_ref, edge_ref, box, loads)
+    copy = pltpu.make_async_copy(parent, parent_ref.at[box], left.at[left.shape[0] - 1])
+    copy.start()
+    return [copy]
+
+
 def middle_kernel(
-    place_ref, gathered_ref, outer_ref, solved_ref, second_ref, far_ref, partial_ref, parent_ref
-):
-    depth = far_ref.shape[1] // 2
-    loads = second_ref.shape[1]
-    partial_ref[...] = dot(far_ref[:, :depth], second_ref[:depth])
-    parent_ref[...] = parent_rows(
-        place_ref, gathered_ref, outer_ref, solved_ref, place_ref[0] & 1, loads
-    )
-
-
-def field_kernel(
-    chunk,
     place_ref,
     gathered_ref,
     outer_ref,
     solved_ref,
-    swapped_ref,
     first_ref,
     second_ref,
     near_ref,
     far_ref,
     near_part_ref,
     far_part_ref,
-    ready_ref,
     field_ref,
     parent_ref,
     pressure,
@@ -226,32 +232,43 @@
     left,
 ):
     mine = place_ref[0] & 1
-    outer, loads = first_ref.shape
-    cells, points = near_ref.shape
-    depth = points // 2
-    cuts = [slice(start, start + chunk) for start in range(0, cells, chunk)]
-    copy = pltpu.make_async_copy(ready_ref, parent_ref.at[mine], left.at[0])
-    copy.start()
-    writes = [copy]
-    turns = (
-        (mine, solved_ref, first_ref, near_ref, near_part_ref),
-        (1 - mine, swapped_ref, second_ref, far_ref, far_part_ref),
-    )
-    for turn, (box, edge_ref, data_ref, operator_ref, part_ref) in enumerate(turns):
-        pressure[turn, : outer - depth] = data_ref[depth:]
-        pressure[turn, outer - depth :] = edge_ref[:, :loads]
-        for cut in cuts:
-            total = part_ref[cut] + dot(operator_ref[cut, depth:], pressure[turn])
-            finished[turn, cut] = total.astype(BF16)
-            copy = pltpu.make_async_copy(
-                finished.at[turn, cut], field_ref.at[box, cut], left.at[len(writes)]
-            )
-            copy.start()
-            writes.append(copy)
-    parent[...] = parent_rows(place_ref, gathered_ref, outer_ref, swapped_ref, 1 - mine, loads)
-    copy = pltpu.make_async_copy(parent, parent_ref.at[1 - mine], left.at[len(writes)])
-    copy.start()
-    writes.append(copy)
+    loads = first_ref.shape[1]
+    depth = far_ref.shape[1] // 2
+    writes = finish_field(
+        mine, solved_ref, first_ref, near_ref, near_part_ref, field_ref, pressure, finished, left
+    )
+    writes += finish_parent(
+        place_ref, gathered_ref, outer_ref, solved_ref, mine, loads, parent_ref, parent, left
+    )
+    far_part_ref[...] = dot(far_ref[:, :depth], second_ref[:depth])
+    finish_copies(writes)
+
+
+def field_kernel(
+    place_ref,
+    gathered_ref,
+    outer_ref,
+    swapped_ref,
+    second_ref,
+    far_ref,
+    far_part_ref,
+    made_field_ref,
+    made_parent_ref,
+    field_ref,
+    parent_ref,
+    pressure,
+    finished,
+    parent,
+    left,
+):
+    other = 1 - (place_ref[0] & 1)
+    loads = second_ref.shape[1]
+    writes = finish_field(
+        other, swapped_ref, second_ref, far_ref, far_part_ref, field_ref, pressure, finished, left
+    )
+    writes += finish_parent(
+        place_ref, gathered_ref, outer_ref, swapped_ref, other, loads, parent_ref, parent, left
+    )
     finish_copies(writes)
 
 
@@ -269,44 +286,36 @@
     operator = in_hbm(solution_op)
     half = jax.ShapeDtypeStruct((outer, loads), BF16)
     part = pltpu.VMEM((cells, loads), F32)
-    own_rows, first = pl.pallas_call(
+    own_rows = pl.pallas_call(
         start_kernel,
-        out_shape=(jax.ShapeDtypeStruct((boxes, local, points), F32), half),
-        in_specs=[SMEM_SPEC, HBM_SPEC, HBM_SPEC],
-        out_specs=(VMEM_SPEC, VMEM_SPEC),
-        scratch_shapes=[pltpu.SemaphoreType.DMA((2,))],
+        out_shape=jax.ShapeDtypeStruct((boxes, local, points), F32),
+        in_specs=[HBM_SPEC],
+        out_specs=VMEM_SPEC,
+        scratch_shapes=[pltpu.SemaphoreType.DMA((1,))],
         compiler_params=pltpu.CompilerParams(vmem_limit_bytes=4 << 20),
         name="start",
-    )(place, whole_map, data)
+    )(whole_map)
     other_rows = exchange(own_rows, "box")
-    first = pl.pallas_call(
-        order_kernel,
-        out_shape=half,
-        in_specs=[ANY_SPEC, ANY_SPEC],
-        out_specs=ANY_SPEC,
-        input_output_aliases={0: 0},
-        compiler_params=pltpu.CompilerParams(vmem_limit_bytes=1 << 20),
-        name="order",
-    )(first, own_rows)
-    crossed = exchange(first, "box")
-    near, near_part, outer_rows, second, far = pl.pallas_call(
+    first, near, near_part, outer_rows, second, far = pl.pallas_call(
         early_kernel,
         out_shape=(
+            half,
             pltpu.VMEM((cells, points), BF16),
             part,
             pltpu.VMEM((boxes, 3, local, points), F32),
             pltpu.VMEM((outer, loads), BF16),
             pltpu.VMEM((cells, points), BF16),
         ),
-        in_specs=[SMEM_SPEC, VMEM_SPEC, HBM_SPEC, HBM_SPEC, HBM_SPEC],
-        out_specs=(VMEM_SPEC,) * 5,
-        scratch_shapes=[pltpu.SemaphoreType.DMA((4,))],
+        in_specs=[SMEM_SPEC, ANY_SPEC, HBM_SPEC, HBM_SPEC, HBM_SPEC],
+        out_specs=(VMEM_SPEC,) * 6,
+        scratch_shapes=[pltpu.SemaphoreType.DMA((5,))],
         compiler_params=pltpu.CompilerParams(vmem_limit_bytes=4 << 20),
         cost_estimate=pl.CostEstimate(
             flops=cells * points * loads, bytes_accessed=6 << 20, transcendentals=0
         ),
         name="early",
-    )(place, first, whole_map, data, operator)
+    )(place, own_rows, whole_map, data, operator)
+    crossed = exchange(first, "box")
     other_rows, near = lax.optimization_barrier((other_rows, near))
     packed = jnp.concatenate(
         [
@@ -331,48 +340,41 @@
         name="solve",
     )(place, gathered, first, crossed)
     swapped = exchange(solved, "row")
-    far_part, ready = pl.pallas_call(
+    outputs = (
+        jax.ShapeDtypeStruct((boxes, cells, loads), BF16),
+        jax.ShapeDtypeStruct((boxes, 3, local, 2 * outer), F32),
+    )
+
+    def scratch(pieces):
+        return [
+            pltpu.VMEM((points - points // 2, loads), BF16),
+            pltpu.VMEM((cells, loads), BF16),
+            pltpu.VMEM((3, local, 2 * outer), F32),
+            pltpu.SemaphoreType.DMA((pieces + 1,)),
+        ]
+
+    far_part, *made = pl.pallas_call(
         middle_kernel,
-        out_shape=(part, pltpu.VMEM((3, local, 2 * outer), F32)),
-        in_specs=[SMEM_SPEC] + [VMEM_SPEC] * 5,
-        out_specs=(VMEM_SPEC,) * 2,
-        compiler_params=pltpu.CompilerParams(vmem_limit_bytes=6 << 20),
+        out_shape=(part,) + outputs,
+        in_specs=[SMEM_SPEC] + [VMEM_SPEC] * 8,
+        out_specs=(VMEM_SPEC, ANY_SPEC, ANY_SPEC),
+        scratch_shapes=scratch(8),
+        compiler_params=pltpu.CompilerParams(vmem_limit_bytes=10 << 20),
         cost_estimate=pl.CostEstimate(
-            flops=cells * points * loads, bytes_accessed=6 << 20, transcendentals=0
+            flops=2 * cells * points * loads, bytes_accessed=6 << 20, transcendentals=0
         ),
         name="middle",
-    )(place, gathered, outer_rows, solved, second, far)
-    chunk = 256
+    )(place, gathered, outer_rows, solved, first, second, near, far, near_part)
     interior_field, parent_map = pl.pallas_call(
-        functools.partial(field_kernel, chunk),
-        out_shape=(
-            jax.ShapeDtypeStruct((boxes, cells, loads), BF16),
-            jax.ShapeDtypeStruct((boxes, 3, local, 2 * outer), F32),
-        ),
-        in_specs=[SMEM_SPEC] + [VMEM_SPEC] * 11,
+        field_kernel,
+        out_shape=outputs,
+        in_specs=[SMEM_SPEC] + [VMEM_SPEC] * 6 + [ANY_SPEC] * 2,
         out_specs=(ANY_SPEC, ANY_SPEC),
-        scratch_shapes=[
-            pltpu.VMEM((boxes, points - points // 2, loads), BF16),
-            pltpu.VMEM((boxes, cells, loads), BF16),
-            pltpu.VMEM((3, local, 2 * outer), F32),
-            pltpu.SemaphoreType.DMA((boxes * cells // chunk + 2,)),
-        ],
-        compiler_params=pltpu.CompilerParams(vmem_limit_bytes=16 << 20),
+        scratch_shapes=scratch(8),
+        input_output_aliases={7: 0, 8: 1},
+        compiler_params=pltpu.CompilerParams(vmem_limit_bytes=10 << 20),
         name="field",
-    )(
-        place,
-        gathered,
-        outer_rows,
-        solved,
-        swapped,
-        first,
-        second,
-        near,
-        far,
-        near_part,
-        far_part,
-        ready,
-    )
+    )(place, gathered, outer_rows, swapped, second, far, far_part, *made)
     return (parent_map, interior_field)
 
 

time: 35.1 us -> 34.7 us (0.989)
    pallas_call x5 -> x4, Pallas kernels: 8.03 us -> 7.89 us  [the longest x1 2.82 us: per_device(): pl.pallas_call(early_kernel, out_shape=(half, pltpu.VMEM((cells, points),...]
  transfers between devices with their start and end apart: 3 -> 3, of which waited for: 1 -> 0; matrix products, arithmetic and copies ran while one was open for 0% -> 0% of each run, Pallas kernels for 11% -> 14%
where the time goes in v6:
time: 34.7 us; the launch traced here: 34.5 us
  blocking collectives  21.7 us (63%)
  Pallas kernels  9.59 us (28%)
  starting transfers between devices  2.48 us (7%)
  between operations  0.7 us (2%)
    all_gather x1, blocking collectives, per_device(): gathered = lax.all_gather(packed, 'row', axis=0)  21.7 us
    pallas_call x1, Pallas kernels, per_device(): pl.pallas_call(early_kernel, out_shape=(half, pltpu.VMEM((cells, points),...  2.82 us
    ppermute x3, starting transfers between devices, exchange(): return lax.ppermute(value, axis, pairs)  2.48 us
    pallas_call x1, Pallas kernels, per_device(): pl.pallas_call(middle_kernel, out_shape=(part,) + outputs, in_specs=[SMEM...  2.14 us
    pallas_call x1, Pallas kernels, per_device(): pl.pallas_call(field_kernel, out_shape=outputs, in_specs=[SMEM_SPEC] + [V...  2.08 us
    pallas_call x1, Pallas kernels, per_device(): pl.pallas_call(solve_kernel, out_shape=jax.ShapeDtypeStruct((edge, loads...  1.69 us
    pallas_call x1, Pallas kernels, per_device(): pl.pallas_call(start_kernel, out_shape=jax.ShapeDtypeStruct((boxes, local...  0.85 us
  transfers between devices with their start and end apart: 3, of which 0 were waited for; matrix products, arithmetic and copies ran while one was open for 0% of the time, Pallas kernels for 14%

profile of v6, /device:TPU:1, one launch (start us, length us, event | category | flops | bytes accessed | tf_op | source)
XLA Modules:
  0.0 34.5 jit_solution(11840948446320510952)
XLA Ops:
  0.6 0.9 %start.1.rows_ref = f32[2,16,512]{2,1,0:T(8,128)S(1)} custom-call(f32[2,4,16,512]{3,2,1,0:T(8,128)} %map_ref.3), custom_call_target="tpu_custom_call" | custom-call | tf_op jit(solution)/shard_map/start/pallas_call | solution.py:289
  1.5 2.1 %collective-permute-start = (f32[2,16,512]{2,1,0:T(8,128)S(1)}, f32[2,16,512]{2,1,0:T(8,128)S(1)}, u32[]{:S(2)}, u32[]{:S(2)}) collective-permute-start(f32[2,16,512]{2,1,0:T(8,128)S(1)} %start.1.rows_ref), channel_id=1, source_target_pairs={{0,8},{8,0},{16,24},{24,16},{32,40},{40,32},{48,56},{56,48},{64,72... | collective-permute-start | bytes 196616 | tf_op jit(solution)/shard_map/ppermute | solution.py:22
  3.6 2.8 %early.1 = (bf16[384,768]{1,0:T(8,128)(2,1)S(1)}, bf16[2048,512]{1,0:T(8,128)(2,1)S(1)}, f32[2048,768]{1,0:T(8,128)S(1)}, f32[2,3,16,512]{3,2,1,0:T(8,128)S(1)},...) custom-call(s32[1]{0:T(128)} %bitcast.place_ref, f32[2,16,512]{2,1,0:T(8,128)S(1)} %start.1.rows_ref, ...), custom_call_target="tpu_custom_call" | custom-call | flops 805306368 | bytes 6291456 | tf_op jit(solution)/shard_map/early/pallas_call | solution.py:299
  6.4 0.1 collective-permute-start.1
  6.6 0.0 collective-permute-done
  6.6 21.7 %all-gather = f32[16,16,896]{2,1,0:T(8,128)S(1)} all-gather(f32[2,16,896]{2,1,0:T(8,128)S(1)} %pad_maximum_fusion), channel_id=2, replica_groups=mesh['box'=32,'row'=8] {'row'}, dimensions={0}, use_global_device_ids=true | all-gather | bytes 1032192 | tf_op jit(solution)/shard_map/all_gather | solution.py:328
  28.3 0.0 collective-permute-done.1.other_ref
  28.3 1.7 %solve.1.solved_ref = bf16[128,1152]{1,0:T(8,128)(2,1)S(1)} custom-call(s32[1]{0:T(128)} %bitcast.place_ref, f32[8,2,16,896]{3,2,1,0:T(8,128)S(1)} %bitcast.3, bf16[384,768]{1,0:T(8,128)(2,1)S(1)} %get-tuple-element.18.own_ref.first_ref, bf16[384,768]{1,0:T(8,128)(2,1)S(1)} %collective-permute-done.1.other_ref), custom_call_target="tpu_custom_call" | custom-call | tf_op jit(solution)/shard_map/solve/pallas_call | solution.py:329
  30.0 0.2 collective-permute-start.2
  30.3 2.1 %middle.1 = (f32[2048,768]{1,0:T(8,128)S(1)}, bf16[2,2048,768]{2,1,0:T(8,128)(2,1)}, f32[2,3,16,768]{3,2,1,0:T(8,128)}) custom-call(s32[1]{0:T(128)} %bitcast.place_ref, f32[8,2,16,896]{3,2,1,0:T(8,128)S(1)} %bitcast.4, f32[2,3,16,512]{3,2,1,0:T(8,128)S(1)} %get-tuple-element.17.outer_ref, bf16[128,1152]{1,0:T(8,128)(2,1)S(1)} %solve.1.solved_ref, ...), custom_call_target="tpu_custom_call" | custom-call | flops 1610612736 | bytes 6291456 | tf_op jit(solution)/shard_map/middle/pallas_call | solution.py:356
  32.4 0.0 collective-permute-done.2.swapped_ref
  32.4 2.1 %field.1 = (bf16[2,2048,768]{2,1,0:T(8,128)(2,1)}, f32[2,3,16,768]{3,2,1,0:T(8,128)}) custom-call(s32[1]{0:T(128)} %bitcast.place_ref, f32[8,2,16,896]{3,2,1,0:T(8,128)S(1)} %bitcast.5, f32[2,3,16,512]{3,2,1,0:T(8,128)S(1)} %get-tuple-element.17.outer_ref, ...), custom_call_target="tpu_custom_call", output_to_operand_aliasing={{0}: (7, {}), {1}: (8, {})} | custom-call | tf_op jit(solution)/shard_map/field/pallas_call | solution.py:368
  (4 shorter events, 0.0 us)
Async XLA Ops:
  1.5 5.1 %collective-permute-start = (f32[2,16,512]{2,1,0:T(8,128)S(1)}, f32[2,16,512]{2,1,0:T(8,128)S(1)}, u32[]{:S(2)}, u32[]{:S(2)}) collective-permute-start(f32[2,16,512]{2,1,0:T(8,128)S(1)} %start.1.rows_ref), channel_id=1, source_target_pairs={{0,8},{8,0},{16,24},{24,16},{32,40},{40,32},{48,56},{56,48},{64,72... | collective-permute-start | bytes 196616 | tf_op jit(solution)/shard_map/ppermute | solution.py:22
  6.4 21.9 %collective-permute-start.1 = (bf16[384,768]{1,0:T(8,128)(2,1)S(1)}, bf16[384,768]{1,0:T(8,128)(2,1)S(1)}, u32[]{:S(2)}, u32[]{:S(2)}) collective-permute-start(bf16[384,768]{1,0:T(8,128)(2,1)S(1)} %get-tuple-element.18.own_ref.first_ref), channel_id=1, source_target_pairs={{0,8},{8,0},{16,24},{24,16},{32,40},{40,32},{48,56},{56,48},{64,72... | collective-permute-start | bytes 1769480 | tf_op jit(solution)/shard_map/ppermute | solution.py:22
  30.0 2.4 %collective-permute-start.2 = (bf16[128,1152]{1,0:T(8,128)(2,1)S(1)}, bf16[128,1152]{1,0:T(8,128)(2,1)S(1)}, u32[]{:S(2)}, u32[]{:S(2)}) collective-permute-start(bf16[128,1152]{1,0:T(8,128)(2,1)S(1)} %solve.1.solved_ref), channel_id=1, source_target_pairs={{0,1},{1,0},{2,3},{3,2},{4,5},{5,4},{6,7},{7,6},{8,9},{9,8},{10,11... | collective-permute-start | bytes 884744 | tf_op jit(solution)/shard_map/ppermute | solution.py:22

commit v7 on v6

--- a/solution.py
+++ b/solution.py
@@ -67,33 +67,54 @@
     copy.wait()
 
 
-def early_kernel(
-    place_ref,
-    rows_ref,
-    map_ref,
-    data_ref,
-    operator_ref,
-    first_ref,
-    near_ref,
-    partial_ref,
-    outer_ref,
-    second_ref,
-    far_ref,
-    arrived,
+def bring_operators(
+    mine, map_ref, data_ref, operator_ref, near_ref, partial_ref, outer_ref, second_ref, far_ref, arrived
 ):
-    mine = place_ref[0] & 1
-    depth = operator_ref.shape[2] // 2
     copies = (
-        pltpu.make_async_copy(data_ref.at[mine], first_ref, arrived.at[0]),
         pltpu.make_async_copy(operator_ref.at[mine], near_ref, arrived.at[1]),
         pltpu.make_async_copy(operator_ref.at[1 - mine], far_ref, arrived.at[2]),
         pltpu.make_async_copy(data_ref.at[1 - mine], second_ref, arrived.at[3]),
         pltpu.make_async_copy(map_ref.at[:, pl.ds(0, 3)], outer_ref, arrived.at[4]),
     )
     start_copies(copies)
-    finish_copies(copies[:2])
-    partial_ref[...] = dot(near_ref[:, :depth], first_ref[:depth])
-    finish_copies(copies[2:])
+
+    def finish(first_ref):
+        depth = operator_ref.shape[2] // 2
+        copies[0].wait()
+        partial_ref[...] = dot(near_ref[:, :depth], first_ref[:depth])
+        finish_copies(copies[1:])
+
+    return finish
+
+
+def early_kernel(
+    place_ref, rows_ref, map_ref, data_ref, operator_ref, first_ref, *refs
+):
+    mine = place_ref[0] & 1
+    arrived = refs[-1]
+    postponed = place_ref[0] >= 4
+    copy = pltpu.make_async_copy(data_ref.at[mine], first_ref, arrived.at[0])
+
+    @pl.when(postponed)
+    def _():
+        copy.start()
+        copy.wait()
+
+    @pl.when(jnp.logical_not(postponed))
+    def _():
+        copy.start()
+        finish = bring_operators(mine, map_ref, data_ref, operator_ref, *refs)
+        copy.wait()
+        finish(first_ref)
+
+
+def late_kernel(place_ref, solved_ref, map_ref, data_ref, operator_ref, first_ref, *refs):
+    @pl.when(place_ref[0] >= 4)
+    def _():
+        finish = bring_operators(
+            place_ref[0] & 1, map_ref, data_ref, operator_ref, *refs[5:]
+        )
+        finish(first_ref)
 
 
 def solve_kernel(
@@ -121,8 +142,12 @@
     norm = jnp.max(size, axis=0, keepdims=True)[0, 0]
 
     coupling = gathered_ref[:, mine, :, edge:].reshape(edge, 2 * outer)
-    parts = dot(jnp.concatenate(split(coupling[:, :outer], 2), axis=0), own_ref[...])
-    parts += dot(jnp.concatenate(split(coupling[:, outer:], 2), axis=0), other_ref[...])
+    pieces = jnp.concatenate(split(coupling, 2), axis=0)
+    block = 2 * edge
+    mixed = jnp.concatenate([own_ref[block:], other_ref[:edge]], axis=0)
+    parts = dot(pieces[:, :block], own_ref[:block])
+    parts += dot(pieces[:, block : 2 * block], mixed)
+    parts += dot(pieces[:, 2 * block :], other_ref[edge:])
     terms = parts[:edge] + parts[edge:]
 
     total = jnp.where(diagonal, 1.0, power)
@@ -180,7 +205,7 @@
     change = split_dot(weights, coupling)
     own = rows[:, :outer] - change[:, :outer]
     other = -change[:, outer:]
-    is_alpha = place_ref[0] < 2
+    is_alpha = (place_ref[0] & 2) == 0
     left = jnp.where(is_alpha, own, other)
     right = jnp.where(is_alpha, other, own)
     return jnp.concatenate([left, right], axis=1).reshape(3, -1, 2 * outer)
@@ -280,7 +305,8 @@
     outer = 3 * edge
     side = lax.axis_index("box") & 1
     core = lax.axis_index("row") & 1
-    place = (2 * side + core).astype(jnp.int32).reshape(1)
+    upper = jnp.where(2 * lax.axis_index("row") >= lax.axis_size("row"), 4, 0)
+    place = (upper + 2 * side + core).astype(jnp.int32).reshape(1)
     whole_map = in_hbm(dtn_map)
     data = in_hbm(boundary_data.reshape(boxes, outer, loads))
     operator = in_hbm(solution_op)
@@ -296,16 +322,16 @@
         name="start",
     )(whole_map)
     other_rows = exchange(own_rows, "box")
-    first, near, near_part, outer_rows, second, far = pl.pallas_call(
+    brought = (
+        pltpu.VMEM((cells, points), BF16),
+        part,
+        pltpu.VMEM((boxes, 3, local, points), F32),
+        pltpu.VMEM((outer, loads), BF16),
+        pltpu.VMEM((cells, points), BF16),
+    )
+    first, near, *others = pl.pallas_call(
         early_kernel,
-        out_shape=(
-            half,
-            pltpu.VMEM((cells, points), BF16),
-            part,
-            pltpu.VMEM((boxes, 3, local, points), F32),
-            pltpu.VMEM((outer, loads), BF16),
-            pltpu.VMEM((cells, points), BF16),
-        ),
+        out_shape=(half,) + brought,
         in_specs=[SMEM_SPEC, ANY_SPEC, HBM_SPEC, HBM_SPEC, HBM_SPEC],
         out_specs=(VMEM_SPEC,) * 6,
         scratch_shapes=[pltpu.SemaphoreType.DMA((5,))],
@@ -340,6 +366,19 @@
         name="solve",
     )(place, gathered, first, crossed)
     swapped = exchange(solved, "row")
+    near, near_part, outer_rows, second, far = pl.pallas_call(
+        late_kernel,
+        out_shape=brought,
+        in_specs=[SMEM_SPEC, ANY_SPEC] + [HBM_SPEC] * 3 + [VMEM_SPEC] * 6,
+        out_specs=(VMEM_SPEC,) * 5,
+        scratch_shapes=[pltpu.SemaphoreType.DMA((5,))],
+        input_output_aliases={order + 6: order for order in range(5)},
+        compiler_params=pltpu.CompilerParams(vmem_limit_bytes=4 << 20),
+        cost_estimate=pl.CostEstimate(
+            flops=cells * points * loads, bytes_accessed=6 << 20, transcendentals=0
+        ),
+        name="late",
+    )(place, solved, whole_map, data, operator, first, near, *others)
     outputs = (
         jax.ShapeDtypeStruct((boxes, cells, loads), BF16),
         jax.ShapeDtypeStruct((boxes, 3, local, 2 * outer), F32),

time: 34.7 us -> 34.5 us (level)
    pallas_call x1 -> x2, Pallas kernels: 2.82 us -> 2.86 us  [the longest x1 2.82 us: per_device(): pl.pallas_call(early_kernel, out_shape=(half,) + brought, in_specs=[SMEM_...]
  transfers between devices with their start and end apart: 3 -> 3, of which waited for: 0 -> 0; matrix products, arithmetic and copies ran while one was open for 0% -> 0% of each run, Pallas kernels for 14% -> 15%
where the time goes in v7:
time: 34.5 us; the launch traced here: 34.3 us
  blocking collectives  21.5 us (62%)
  Pallas kernels  9.59 us (28%)
  starting transfers between devices  2.48 us (7%)
  between operations  0.71 us (2%)
    all_gather x1, blocking collectives, per_device(): gathered = lax.all_gather(packed, 'row', axis=0)  21.5 us
    pallas_call x1, Pallas kernels, per_device(): pl.pallas_call(early_kernel, out_shape=(half,) + brought, in_specs=[SMEM_...  2.82 us
    ppermute x3, starting transfers between devices, exchange(): return lax.ppermute(value, axis, pairs)  2.48 us
    pallas_call x1, Pallas kernels, per_device(): pl.pallas_call(middle_kernel, out_shape=(part,) + outputs, in_specs=[SMEM...  2.15 us
    pallas_call x1, Pallas kernels, per_device(): pl.pallas_call(field_kernel, out_shape=outputs, in_specs=[SMEM_SPEC] + [V...  2.08 us
    pallas_call x1, Pallas kernels, per_device(): pl.pallas_call(solve_kernel, out_shape=jax.ShapeDtypeStruct((edge, loads...  1.65 us
    pallas_call x1, Pallas kernels, per_device(): pl.pallas_call(start_kernel, out_shape=jax.ShapeDtypeStruct((boxes, local...  0.85 us
  transfers between devices with their start and end apart: 3, of which 0 were waited for; matrix products, arithmetic and copies ran while one was open for 0% of the time, Pallas kernels for 15%

profile of v7, /device:TPU:1, one launch (start us, length us, event | category | flops | bytes accessed | tf_op | source)
XLA Modules:
  0.0 34.3 jit_solution(7183277895519337827)
XLA Ops:
  0.6 0.9 %start.1.rows_ref = f32[2,16,512]{2,1,0:T(8,128)S(1)} custom-call(f32[2,4,16,512]{3,2,1,0:T(8,128)} %map_ref.5), custom_call_target="tpu_custom_call" | custom-call | tf_op jit(solution)/shard_map/start/pallas_call | solution.py:315
  1.5 2.1 %collective-permute-start = (f32[2,16,512]{2,1,0:T(8,128)S(1)}, f32[2,16,512]{2,1,0:T(8,128)S(1)}, u32[]{:S(2)}, u32[]{:S(2)}) collective-permute-start(f32[2,16,512]{2,1,0:T(8,128)S(1)} %start.1.rows_ref), channel_id=1, source_target_pairs={{0,8},{8,0},{16,24},{24,16},{32,40},{40,32},{48,56},{56,48},{64,72... | collective-permute-start | bytes 196616 | tf_op jit(solution)/shard_map/ppermute | solution.py:22
  3.6 2.8 %early.1 = (bf16[384,768]{1,0:T(8,128)(2,1)S(1)}, bf16[2048,512]{1,0:T(8,128)(2,1)S(1)}, f32[2048,768]{1,0:T(8,128)S(1)}, f32[2,3,16,512]{3,2,1,0:T(8,128)S(1)},...) custom-call(s32[1]{0:T(128)} %bitcast.place_ref, f32[2,16,512]{2,1,0:T(8,128)S(1)} %start.1.rows_ref, ...), custom_call_target="tpu_custom_call" | custom-call | flops 805306368 | bytes 6291456 | tf_op jit(solution)/shard_map/early/pallas_call | solution.py:332
  6.4 0.1 collective-permute-start.1
  6.6 0.0 collective-permute-done
  6.6 21.5 %all-gather = f32[16,16,896]{2,1,0:T(8,128)S(1)} all-gather(f32[2,16,896]{2,1,0:T(8,128)S(1)} %pad_maximum_fusion), channel_id=2, replica_groups=mesh['box'=32,'row'=8] {'row'}, dimensions={0}, use_global_device_ids=true | all-gather | bytes 1032192 | tf_op jit(solution)/shard_map/all_gather | solution.py:354
  28.1 0.0 collective-permute-done.1.other_ref
  28.1 1.7 %solve.1.solved_ref = bf16[128,1152]{1,0:T(8,128)(2,1)S(1)} custom-call(s32[1]{0:T(128)} %bitcast.place_ref, f32[8,2,16,896]{3,2,1,0:T(8,128)S(1)} %bitcast.3, bf16[384,768]{1,0:T(8,128)(2,1)S(1)} %get-tuple-element.22.own_ref.first_ref, bf16[384,768]{1,0:T(8,128)(2,1)S(1)} %collective-permute-done.1.other_ref), custom_call_target="tpu_custom_call" | custom-call | tf_op jit(solution)/shard_map/solve/pallas_call | solution.py:355
  29.7 0.2 collective-permute-start.2
  30.0 2.1 %middle.1 = (f32[2048,768]{1,0:T(8,128)S(1)}, bf16[2,2048,768]{2,1,0:T(8,128)(2,1)}, f32[2,3,16,768]{3,2,1,0:T(8,128)}) custom-call(s32[1]{0:T(128)} %bitcast.place_ref, f32[8,2,16,896]{3,2,1,0:T(8,128)S(1)} %bitcast.4, f32[2,3,16,512]{3,2,1,0:T(8,128)S(1)} %get-tuple-element.28.outer_ref, bf16[128,1152]{1,0:T(8,128)(2,1)S(1)} %solve.1.solved_ref, ...), custom_call_target="tpu_custom_call" | custom-call | flops 1610612736 | bytes 6291456 | tf_op jit(solution)/shard_map/middle/pallas_call | solution.py:395
  32.2 0.0 collective-permute-done.2.swapped_ref
  32.2 2.1 %field.1 = (bf16[2,2048,768]{2,1,0:T(8,128)(2,1)}, f32[2,3,16,768]{3,2,1,0:T(8,128)}) custom-call(s32[1]{0:T(128)} %bitcast.place_ref, f32[8,2,16,896]{3,2,1,0:T(8,128)S(1)} %bitcast.5, f32[2,3,16,512]{3,2,1,0:T(8,128)S(1)} %get-tuple-element.28.outer_ref, ...), custom_call_target="tpu_custom_call", output_to_operand_aliasing={{0}: (7, {}), {1}: (8, {})} | custom-call | tf_op jit(solution)/shard_map/field/pallas_call | solution.py:407
  (5 shorter events, 0.1 us)
Async XLA Ops:
  1.5 5.1 %collective-permute-start = (f32[2,16,512]{2,1,0:T(8,128)S(1)}, f32[2,16,512]{2,1,0:T(8,128)S(1)}, u32[]{:S(2)}, u32[]{:S(2)}) collective-permute-start(f32[2,16,512]{2,1,0:T(8,128)S(1)} %start.1.rows_ref), channel_id=1, source_target_pairs={{0,8},{8,0},{16,24},{24,16},{32,40},{40,32},{48,56},{56,48},{64,72... | collective-permute-start | bytes 196616 | tf_op jit(solution)/shard_map/ppermute | solution.py:22
  6.4 21.6 %collective-permute-start.1 = (bf16[384,768]{1,0:T(8,128)(2,1)S(1)}, bf16[384,768]{1,0:T(8,128)(2,1)S(1)}, u32[]{:S(2)}, u32[]{:S(2)}) collective-permute-start(bf16[384,768]{1,0:T(8,128)(2,1)S(1)} %get-tuple-element.22.own_ref.first_ref), channel_id=1, source_target_pairs={{0,8},{8,0},{16,24},{24,16},{32,40},{40,32},{48,56},{56,48},{64,72... | collective-permute-start | bytes 1769480 | tf_op jit(solution)/shard_map/ppermute | solution.py:22
  29.7 2.5 %collective-permute-start.2 = (bf16[128,1152]{1,0:T(8,128)(2,1)S(1)}, bf16[128,1152]{1,0:T(8,128)(2,1)S(1)}, u32[]{:S(2)}, u32[]{:S(2)}) collective-permute-start(bf16[128,1152]{1,0:T(8,128)(2,1)S(1)} %solve.1.solved_ref), channel_id=1, source_target_pairs={{0,1},{1,0},{2,3},{3,2},{4,5},{5,4},{6,7},{7,6},{8,9},{9,8},{10,11... | collective-permute-start | bytes 884744 | tf_op jit(solution)/shard_map/ppermute | solution.py:22

commit v8 on v7

--- a/solution.py
+++ b/solution.py
@@ -67,54 +67,80 @@
     copy.wait()
 
 
-def bring_operators(
-    mine, map_ref, data_ref, operator_ref, near_ref, partial_ref, outer_ref, second_ref, far_ref, arrived
-):
-    copies = (
-        pltpu.make_async_copy(operator_ref.at[mine], near_ref, arrived.at[1]),
+def far_copies(mine, map_ref, data_ref, operator_ref, outer_ref, second_ref, far_ref, arrived):
+    return (
         pltpu.make_async_copy(operator_ref.at[1 - mine], far_ref, arrived.at[2]),
         pltpu.make_async_copy(data_ref.at[1 - mine], second_ref, arrived.at[3]),
         pltpu.make_async_copy(map_ref.at[:, pl.ds(0, 3)], outer_ref, arrived.at[4]),
     )
-    start_copies(copies)
-
-    def finish(first_ref):
-        depth = operator_ref.shape[2] // 2
-        copies[0].wait()
-        partial_ref[...] = dot(near_ref[:, :depth], first_ref[:depth])
-        finish_copies(copies[1:])
-
-    return finish
+
+
+def first_product(first_ref, near_ref, partial_ref):
+    depth = near_ref.shape[1] // 2
+    partial_ref[...] = dot(near_ref[:, :depth], first_ref[:depth])
 
 
 def early_kernel(
-    place_ref, rows_ref, map_ref, data_ref, operator_ref, first_ref, *refs
+    place_ref,
+    rows_ref,
+    map_ref,
+    data_ref,
+    operator_ref,
+    first_ref,
+    near_ref,
+    partial_ref,
+    outer_ref,
+    second_ref,
+    far_ref,
+    arrived,
 ):
     mine = place_ref[0] & 1
-    arrived = refs[-1]
-    postponed = place_ref[0] >= 4
-    copy = pltpu.make_async_copy(data_ref.at[mine], first_ref, arrived.at[0])
-
-    @pl.when(postponed)
-    def _():
-        copy.start()
-        copy.wait()
-
-    @pl.when(jnp.logical_not(postponed))
-    def _():
-        copy.start()
-        finish = bring_operators(mine, map_ref, data_ref, operator_ref, *refs)
-        copy.wait()
-        finish(first_ref)
+    level = place_ref[0] // 4
+    data_copy = pltpu.make_async_copy(data_ref.at[mine], first_ref, arrived.at[0])
+    near_copy = pltpu.make_async_copy(operator_ref.at[mine], near_ref, arrived.at[1])
+
+    @pl.when(level == 0)
+    def _():
+        copies = far_copies(
+            mine, map_ref, data_ref, operator_ref, outer_ref, second_ref, far_ref, arrived
+        )
+        start_copies((data_copy, near_copy) + copies)
+        finish_copies((data_copy, near_copy))
+        first_product(first_ref, near_ref, partial_ref)
+        finish_copies(copies)
+
+    @pl.when(level == 1)
+    def _():
+        start_copies((data_copy, near_copy))
+        finish_copies((data_copy, near_copy))
+
+    @pl.when(level == 2)
+    def _():
+        data_copy.start()
+        data_copy.wait()
 
 
 def late_kernel(place_ref, solved_ref, map_ref, data_ref, operator_ref, first_ref, *refs):
-    @pl.when(place_ref[0] >= 4)
-    def _():
-        finish = bring_operators(
-            place_ref[0] & 1, map_ref, data_ref, operator_ref, *refs[5:]
-        )
-        finish(first_ref)
+    near_ref, partial_ref, outer_ref, second_ref, far_ref, arrived = refs[5:]
+    mine = place_ref[0] & 1
+    level = place_ref[0] // 4
+    copies = far_copies(
+        mine, map_ref, data_ref, operator_ref, outer_ref, second_ref, far_ref, arrived
+    )
+
+    @pl.when(level == 1)
+    def _():
+        start_copies(copies)
+        first_product(first_ref, near_ref, partial_ref)
+        finish_copies(copies)
+
+    @pl.when(level == 2)
+    def _():
+        near_copy = pltpu.make_async_copy(operator_ref.at[mine], near_ref, arrived.at[1])
+        start_copies((near_copy,) + copies)
+        near_copy.wait()
+        first_product(first_ref, near_ref, partial_ref)
+        finish_copies(copies)
 
 
 def solve_kernel(
@@ -305,8 +331,9 @@
     outer = 3 * edge
     side = lax.axis_index("box") & 1
     core = lax.axis_index("row") & 1
-    upper = jnp.where(2 * lax.axis_index("row") >= lax.axis_size("row"), 4, 0)
-    place = (upper + 2 * side + core).astype(jnp.int32).reshape(1)
+    quarter = 4 * lax.axis_index("row") // lax.axis_size("row")
+    level = jnp.minimum(quarter, 2)
+    place = (4 * level + 2 * side + core).astype(jnp.int32).reshape(1)
     whole_map = in_hbm(dtn_map)
     data = in_hbm(boundary_data.reshape(boxes, outer, loads))
     operator = in_hbm(solution_op)

time: 34.5 us -> 34.5 us (level)
  no operation moved by 1% of the time
where the time goes in v8:
time: 34.5 us; the launch traced here: 34.3 us
  blocking collectives  21.4 us (62%)
  Pallas kernels  9.59 us (28%)
  starting transfers between devices  2.5 us (7%)
  between operations  0.71 us (2%)
    all_gather x1, blocking collectives, per_device(): gathered = lax.all_gather(packed, 'row', axis=0)  21.4 us
    pallas_call x1, Pallas kernels, per_device(): pl.pallas_call(early_kernel, out_shape=(half,) + brought, in_specs=[SMEM_...  2.82 us
    ppermute x3, starting transfers between devices, exchange(): return lax.ppermute(value, axis, pairs)  2.5 us
    pallas_call x1, Pallas kernels, per_device(): pl.pallas_call(middle_kernel, out_shape=(part,) + outputs, in_specs=[SMEM...  2.15 us
    pallas_call x1, Pallas kernels, per_device(): pl.pallas_call(field_kernel, out_shape=outputs, in_specs=[SMEM_SPEC] + [V...  2.08 us
    pallas_call x1, Pallas kernels, per_device(): pl.pallas_call(solve_kernel, out_shape=jax.ShapeDtypeStruct((edge, loads...  1.65 us
    pallas_call x1, Pallas kernels, per_device(): pl.pallas_call(start_kernel, out_shape=jax.ShapeDtypeStruct((boxes, local...  0.85 us
  transfers between devices with their start and end apart: 3, of which 0 were waited for; matrix products, arithmetic and copies ran while one was open for 0% of the time, Pallas kernels for 15%

profile of v8, /device:TPU:1, one launch (start us, length us, event | category | flops | bytes accessed | tf_op | source)
XLA Modules:
  0.0 34.3 jit_solution(1998646187993399650)
XLA Ops:
  0.6 0.9 %start.1.rows_ref = f32[2,16,512]{2,1,0:T(8,128)S(1)} custom-call(f32[2,4,16,512]{3,2,1,0:T(8,128)} %map_ref.5), custom_call_target="tpu_custom_call" | custom-call | tf_op jit(solution)/shard_map/start/pallas_call | solution.py:342
  1.5 2.1 %collective-permute-start = (f32[2,16,512]{2,1,0:T(8,128)S(1)}, f32[2,16,512]{2,1,0:T(8,128)S(1)}, u32[]{:S(2)}, u32[]{:S(2)}) collective-permute-start(f32[2,16,512]{2,1,0:T(8,128)S(1)} %start.1.rows_ref), channel_id=1, source_target_pairs={{0,8},{8,0},{16,24},{24,16},{32,40},{40,32},{48,56},{56,48},{64,72... | collective-permute-start | bytes 196616 | tf_op jit(solution)/shard_map/ppermute | solution.py:22
  3.6 2.8 %early.1 = (bf16[384,768]{1,0:T(8,128)(2,1)S(1)}, bf16[2048,512]{1,0:T(8,128)(2,1)S(1)}, f32[2048,768]{1,0:T(8,128)S(1)}, f32[2,3,16,512]{3,2,1,0:T(8,128)S(1)},...) custom-call(s32[1]{0:T(128)} %bitcast.place_ref, f32[2,16,512]{2,1,0:T(8,128)S(1)} %start.1.rows_ref, ...), custom_call_target="tpu_custom_call" | custom-call | flops 805306368 | bytes 6291456 | tf_op jit(solution)/shard_map/early/pallas_call | solution.py:359
  6.4 0.1 collective-permute-start.1
  6.6 0.0 collective-permute-done
  6.6 21.4 %all-gather = f32[16,16,896]{2,1,0:T(8,128)S(1)} all-gather(f32[2,16,896]{2,1,0:T(8,128)S(1)} %pad_maximum_fusion), channel_id=2, replica_groups=mesh['box'=32,'row'=8] {'row'}, dimensions={0}, use_global_device_ids=true | all-gather | bytes 1032192 | tf_op jit(solution)/shard_map/all_gather | solution.py:381
  28.1 0.0 collective-permute-done.1.other_ref
  28.1 1.7 %solve.1.solved_ref = bf16[128,1152]{1,0:T(8,128)(2,1)S(1)} custom-call(s32[1]{0:T(128)} %bitcast.place_ref, f32[8,2,16,896]{3,2,1,0:T(8,128)S(1)} %bitcast.3, bf16[384,768]{1,0:T(8,128)(2,1)S(1)} %get-tuple-element.22.own_ref.first_ref, bf16[384,768]{1,0:T(8,128)(2,1)S(1)} %collective-permute-done.1.other_ref), custom_call_target="tpu_custom_call" | custom-call | tf_op jit(solution)/shard_map/solve/pallas_call | solution.py:382
  29.7 0.2 collective-permute-start.2
  30.0 2.1 %middle.1 = (f32[2048,768]{1,0:T(8,128)S(1)}, bf16[2,2048,768]{2,1,0:T(8,128)(2,1)}, f32[2,3,16,768]{3,2,1,0:T(8,128)}) custom-call(s32[1]{0:T(128)} %bitcast.place_ref, f32[8,2,16,896]{3,2,1,0:T(8,128)S(1)} %bitcast.4, f32[2,3,16,512]{3,2,1,0:T(8,128)S(1)} %get-tuple-element.28.outer_ref, bf16[128,1152]{1,0:T(8,128)(2,1)S(1)} %solve.1.solved_ref, ...), custom_call_target="tpu_custom_call" | custom-call | flops 1610612736 | bytes 6291456 | tf_op jit(solution)/shard_map/middle/pallas_call | solution.py:422
  32.2 0.0 collective-permute-done.2.swapped_ref
  32.2 2.1 %field.1 = (bf16[2,2048,768]{2,1,0:T(8,128)(2,1)}, f32[2,3,16,768]{3,2,1,0:T(8,128)}) custom-call(s32[1]{0:T(128)} %bitcast.place_ref, f32[8,2,16,896]{3,2,1,0:T(8,128)S(1)} %bitcast.5, f32[2,3,16,512]{3,2,1,0:T(8,128)S(1)} %get-tuple-element.28.outer_ref, ...), custom_call_target="tpu_custom_call", output_to_operand_aliasing={{0}: (7, {}), {1}: (8, {})} | custom-call | tf_op jit(solution)/shard_map/field/pallas_call | solution.py:434
  (5 shorter events, 0.1 us)
Async XLA Ops:
  1.5 5.1 %collective-permute-start = (f32[2,16,512]{2,1,0:T(8,128)S(1)}, f32[2,16,512]{2,1,0:T(8,128)S(1)}, u32[]{:S(2)}, u32[]{:S(2)}) collective-permute-start(f32[2,16,512]{2,1,0:T(8,128)S(1)} %start.1.rows_ref), channel_id=1, source_target_pairs={{0,8},{8,0},{16,24},{24,16},{32,40},{40,32},{48,56},{56,48},{64,72... | collective-permute-start | bytes 196616 | tf_op jit(solution)/shard_map/ppermute | solution.py:22
  6.4 21.6 %collective-permute-start.1 = (bf16[384,768]{1,0:T(8,128)(2,1)S(1)}, bf16[384,768]{1,0:T(8,128)(2,1)S(1)}, u32[]{:S(2)}, u32[]{:S(2)}) collective-permute-start(bf16[384,768]{1,0:T(8,128)(2,1)S(1)} %get-tuple-element.22.own_ref.first_ref), channel_id=1, source_target_pairs={{0,8},{8,0},{16,24},{24,16},{32,40},{40,32},{48,56},{56,48},{64,72... | collective-permute-start | bytes 1769480 | tf_op jit(solution)/shard_map/ppermute | solution.py:22
  29.7 2.5 %collective-permute-start.2 = (bf16[128,1152]{1,0:T(8,128)(2,1)S(1)}, bf16[128,1152]{1,0:T(8,128)(2,1)S(1)}, u32[]{:S(2)}, u32[]{:S(2)}) collective-permute-start(bf16[128,1152]{1,0:T(8,128)(2,1)S(1)} %solve.1.solved_ref), channel_id=1, source_target_pairs={{0,1},{1,0},{2,3},{3,2},{4,5},{5,4},{6,7},{7,6},{8,9},{9,8},{10,11... | collective-permute-start | bytes 884744 | tf_op jit(solution)/shard_map/ppermute | solution.py:22

commit v9 on v8

--- a/solution.py
+++ b/solution.py
@@ -114,11 +114,6 @@
         start_copies((data_copy, near_copy))
         finish_copies((data_copy, near_copy))
 
-    @pl.when(level == 2)
-    def _():
-        data_copy.start()
-        data_copy.wait()
-
 
 def late_kernel(place_ref, solved_ref, map_ref, data_ref, operator_ref, first_ref, *refs):
     near_ref, partial_ref, outer_ref, second_ref, far_ref, arrived = refs[5:]
@@ -131,14 +126,6 @@
     @pl.when(level == 1)
     def _():
         start_copies(copies)
-        first_product(first_ref, near_ref, partial_ref)
-        finish_copies(copies)
-
-    @pl.when(level == 2)
-    def _():
-        near_copy = pltpu.make_async_copy(operator_ref.at[mine], near_ref, arrived.at[1])
-        start_copies((near_copy,) + copies)
-        near_copy.wait()
         first_product(first_ref, near_ref, partial_ref)
         finish_copies(copies)
 
@@ -332,7 +319,7 @@
     side = lax.axis_index("box") & 1
     core = lax.axis_index("row") & 1
     quarter = 4 * lax.axis_index("row") // lax.axis_size("row")
-    level = jnp.minimum(quarter, 2)
+    level = jnp.minimum(quarter, 1)
     place = (4 * level + 2 * side + core).astype(jnp.int32).reshape(1)
     whole_map = in_hbm(dtn_map)
     data = in_hbm(boundary_data.reshape(boxes, outer, loads))

time: 34.5 us -> 33.9 us (0.983)
  blocking collectives: 21.4 us -> 20.9 us
    all_gather x1, blocking collectives: 21.4 us -> 20.9 us  [per_device(): gathered = lax.all_gather(packed, 'row', axis=0)]
where the time goes in v9:
time: 33.9 us; the launch traced here: 33.7 us
  blocking collectives  20.9 us (62%)
  Pallas kernels  9.59 us (28%)
  starting transfers between devices  2.5 us (7%)
  between operations  0.71 us (2%)
    all_gather x1, blocking collectives, per_device(): gathered = lax.all_gather(packed, 'row', axis=0)  20.9 us
    pallas_call x1, Pallas kernels, per_device(): pl.pallas_call(early_kernel, out_shape=(half,) + brought, in_specs=[SMEM_...  2.82 us
    ppermute x3, starting transfers between devices, exchange(): return lax.ppermute(value, axis, pairs)  2.5 us
    pallas_call x1, Pallas kernels, per_device(): pl.pallas_call(middle_kernel, out_shape=(part,) + outputs, in_specs=[SMEM...  2.15 us
    pallas_call x1, Pallas kernels, per_device(): pl.pallas_call(field_kernel, out_shape=outputs, in_specs=[SMEM_SPEC] + [V...  2.08 us
    pallas_call x1, Pallas kernels, per_device(): pl.pallas_call(solve_kernel, out_shape=jax.ShapeDtypeStruct((edge, loads...  1.65 us
    pallas_call x1, Pallas kernels, per_device(): pl.pallas_call(start_kernel, out_shape=jax.ShapeDtypeStruct((boxes, local...  0.85 us
  transfers between devices with their start and end apart: 3, of which 0 were waited for; matrix products, arithmetic and copies ran while one was open for 0% of the time, Pallas kernels for 15%

profile of v9, /device:TPU:1, one launch (start us, length us, event | category | flops | bytes accessed | tf_op | source)
XLA Modules:
  0.0 33.7 jit_solution(16094997450147535188)
XLA Ops:
  0.6 0.9 %start.1.rows_ref = f32[2,16,512]{2,1,0:T(8,128)S(1)} custom-call(f32[2,4,16,512]{3,2,1,0:T(8,128)} %map_ref.5), custom_call_target="tpu_custom_call" | custom-call | tf_op jit(solution)/shard_map/start/pallas_call | solution.py:329
  1.5 2.1 %collective-permute-start = (f32[2,16,512]{2,1,0:T(8,128)S(1)}, f32[2,16,512]{2,1,0:T(8,128)S(1)}, u32[]{:S(2)}, u32[]{:S(2)}) collective-permute-start(f32[2,16,512]{2,1,0:T(8,128)S(1)} %start.1.rows_ref), channel_id=1, source_target_pairs={{0,8},{8,0},{16,24},{24,16},{32,40},{40,32},{48,56},{56,48},{64,72... | collective-permute-start | bytes 196616 | tf_op jit(solution)/shard_map/ppermute | solution.py:22
  3.6 2.8 %early.1 = (bf16[384,768]{1,0:T(8,128)(2,1)S(1)}, bf16[2048,512]{1,0:T(8,128)(2,1)S(1)}, f32[2048,768]{1,0:T(8,128)S(1)}, f32[2,3,16,512]{3,2,1,0:T(8,128)S(1)},...) custom-call(s32[1]{0:T(128)} %bitcast.place_ref, f32[2,16,512]{2,1,0:T(8,128)S(1)} %start.1.rows_ref, ...), custom_call_target="tpu_custom_call" | custom-call | flops 805306368 | bytes 6291456 | tf_op jit(solution)/shard_map/early/pallas_call | solution.py:346
  6.4 0.1 collective-permute-start.1
  6.6 0.0 collective-permute-done
  6.6 20.9 %all-gather = f32[16,16,896]{2,1,0:T(8,128)S(1)} all-gather(f32[2,16,896]{2,1,0:T(8,128)S(1)} %pad_maximum_fusion), channel_id=2, replica_groups=mesh['box'=32,'row'=8] {'row'}, dimensions={0}, use_global_device_ids=true | all-gather | bytes 1032192 | tf_op jit(solution)/shard_map/all_gather | solution.py:368
  27.5 0.0 collective-permute-done.1.other_ref
  27.5 1.6 %solve.1.solved_ref = bf16[128,1152]{1,0:T(8,128)(2,1)S(1)} custom-call(s32[1]{0:T(128)} %bitcast.place_ref, f32[8,2,16,896]{3,2,1,0:T(8,128)S(1)} %bitcast.3, bf16[384,768]{1,0:T(8,128)(2,1)S(1)} %get-tuple-element.22.own_ref.first_ref, bf16[384,768]{1,0:T(8,128)(2,1)S(1)} %collective-permute-done.1.other_ref), custom_call_target="tpu_custom_call" | custom-call | tf_op jit(solution)/shard_map/solve/pallas_call | solution.py:369
  29.2 0.2 collective-permute-start.2
  29.5 2.1 %middle.1 = (f32[2048,768]{1,0:T(8,128)S(1)}, bf16[2,2048,768]{2,1,0:T(8,128)(2,1)}, f32[2,3,16,768]{3,2,1,0:T(8,128)}) custom-call(s32[1]{0:T(128)} %bitcast.place_ref, f32[8,2,16,896]{3,2,1,0:T(8,128)S(1)} %bitcast.4, f32[2,3,16,512]{3,2,1,0:T(8,128)S(1)} %get-tuple-element.28.outer_ref, bf16[128,1152]{1,0:T(8,128)(2,1)S(1)} %solve.1.solved_ref, ...), custom_call_target="tpu_custom_call" | custom-call | flops 1610612736 | bytes 6291456 | tf_op jit(solution)/shard_map/middle/pallas_call | solution.py:409
  31.6 0.0 collective-permute-done.2.swapped_ref
  31.7 2.1 %field.1 = (bf16[2,2048,768]{2,1,0:T(8,128)(2,1)}, f32[2,3,16,768]{3,2,1,0:T(8,128)}) custom-call(s32[1]{0:T(128)} %bitcast.place_ref, f32[8,2,16,896]{3,2,1,0:T(8,128)S(1)} %bitcast.5, f32[2,3,16,512]{3,2,1,0:T(8,128)S(1)} %get-tuple-element.28.outer_ref, ...), custom_call_target="tpu_custom_call", output_to_operand_aliasing={{0}: (7, {}), {1}: (8, {})} | custom-call | tf_op jit(solution)/shard_map/field/pallas_call | solution.py:421
  (5 shorter events, 0.1 us)
Async XLA Ops:
  1.5 5.1 %collective-permute-start = (f32[2,16,512]{2,1,0:T(8,128)S(1)}, f32[2,16,512]{2,1,0:T(8,128)S(1)}, u32[]{:S(2)}, u32[]{:S(2)}) collective-permute-start(f32[2,16,512]{2,1,0:T(8,128)S(1)} %start.1.rows_ref), channel_id=1, source_target_pairs={{0,8},{8,0},{16,24},{24,16},{32,40},{40,32},{48,56},{56,48},{64,72... | collective-permute-start | bytes 196616 | tf_op jit(solution)/shard_map/ppermute | solution.py:22
  6.4 21.1 %collective-permute-start.1 = (bf16[384,768]{1,0:T(8,128)(2,1)S(1)}, bf16[384,768]{1,0:T(8,128)(2,1)S(1)}, u32[]{:S(2)}, u32[]{:S(2)}) collective-permute-start(bf16[384,768]{1,0:T(8,128)(2,1)S(1)} %get-tuple-element.22.own_ref.first_ref), channel_id=1, source_target_pairs={{0,8},{8,0},{16,24},{24,16},{32,40},{40,32},{48,56},{56,48},{64,72... | collective-permute-start | bytes 1769480 | tf_op jit(solution)/shard_map/ppermute | solution.py:22
  29.2 2.5 %collective-permute-start.2 = (bf16[128,1152]{1,0:T(8,128)(2,1)S(1)}, bf16[128,1152]{1,0:T(8,128)(2,1)S(1)}, u32[]{:S(2)}, u32[]{:S(2)}) collective-permute-start(bf16[128,1152]{1,0:T(8,128)(2,1)S(1)} %solve.1.solved_ref), channel_id=1, source_target_pairs={{0,1},{1,0},{2,3},{3,2},{4,5},{5,4},{6,7},{7,6},{8,9},{9,8},{10,11... | collective-permute-start | bytes 884744 | tf_op jit(solution)/shard_map/ppermute | solution.py:22

commit v10 on v9

--- a/solution.py
+++ b/solution.py
@@ -138,7 +138,6 @@
     solved_ref,
     sums,
     power_ref,
-    terms_ref,
 ):
     mine = place_ref[0] & 1
     edge = sums.shape[0]
@@ -151,6 +150,7 @@
     scale = 1.0 / jnp.sum(kept, axis=1, keepdims=True)
     right_scale = 1.0 / jnp.sum(kept, axis=0, keepdims=True)
     power = jnp.where(diagonal, 0.0, -shared) * scale
+    power_ref[...] = power
     size = jnp.sum(jnp.abs(power), axis=1, keepdims=True)
     norm = jnp.max(size, axis=0, keepdims=True)[0, 0]
 
@@ -170,25 +170,21 @@
         total = total + both[:edge]
         power = both[edge:]
     total = total + split_dot(total, power)
-    sums[...] = total
-    power_ref[...] = power
-    terms_ref[...] = terms
-
-    def hand_out(total, terms):
-        inverse = total * right_scale
-        solved_ref[:, :loads] = (-split_dot(inverse, terms)).astype(BF16)
+
+    def hand_out(inverse, values):
+        solved_ref[:, :loads] = (-values).astype(BF16)
         for order, piece in enumerate(split(inverse, 3)):
             solved_ref[:, loads + order * edge : loads + (order + 1) * edge] = piece
 
-    hand_out(total, terms)
+    inverse = total * right_scale
+    hand_out(inverse, split_dot(inverse, terms))
     bound = norm
     for _ in range(SURE_DOUBLINGS + 1):
         bound = bound * bound
 
     @pl.when(bound > REMAINDER)
     def _():
-        last = power_ref[...]
-        power_ref[...] = full_dot(last, last)
+        sums[...] = jnp.where(diagonal, 1.0, 0.0)
 
         def more(carry):
             left, count = carry
@@ -202,8 +198,12 @@
             power_ref[...] = both[edge:]
             return left * left, count + 1
 
-        lax.while_loop(more, double, (bound, jnp.int32(0)))
-        hand_out(sums[...], terms_ref[...])
+        lax.while_loop(more, double, (norm, jnp.int32(0)))
+        fine = dot(jnp.concatenate(split(coupling[:, :outer], 3), axis=0), own_ref[...])
+        fine += dot(jnp.concatenate(split(coupling[:, outer:], 3), axis=0), other_ref[...])
+        exact = fine[:edge] + (fine[edge : 2 * edge] + fine[2 * edge :])
+        inverse = sums[...] * right_scale
+        hand_out(inverse, full_dot(inverse, exact))
 
 
 def parent_rows(place_ref, gathered_ref, outer_ref, solved_ref, box, loads):
@@ -374,7 +374,6 @@
         scratch_shapes=[
             pltpu.VMEM((edge, edge), F32),
             pltpu.VMEM((edge, edge), F32),
-            pltpu.VMEM((edge, loads), F32),
         ],
         compiler_params=pltpu.CompilerParams(vmem_limit_bytes=12 << 20),
         name="solve",

time: 33.9 us -> 33.9 us (level)
  no operation moved by 1% of the time
where the time goes in v10:
time: 33.9 us; the launch traced here: 33.7 us
  blocking collectives  20.9 us (62%)
  Pallas kernels  9.59 us (28%)
  starting transfers between devices  2.49 us (7%)
  between operations  0.7 us (2%)
    all_gather x1, blocking collectives, per_device(): gathered = lax.all_gather(packed, 'row', axis=0)  20.9 us
    pallas_call x1, Pallas kernels, per_device(): pl.pallas_call(early_kernel, out_shape=(half,) + brought, in_specs=[SMEM_...  2.82 us
    ppermute x3, starting transfers between devices, exchange(): return lax.ppermute(value, axis, pairs)  2.49 us
    pallas_call x1, Pallas kernels, per_device(): pl.pallas_call(middle_kernel, out_shape=(part,) + outputs, in_specs=[SMEM...  2.15 us
    pallas_call x1, Pallas kernels, per_device(): pl.pallas_call(field_kernel, out_shape=outputs, in_specs=[SMEM_SPEC] + [V...  2.08 us
    pallas_call x1, Pallas kernels, per_device(): pl.pallas_call(solve_kernel, out_shape=jax.ShapeDtypeStruct((edge, loads...  1.65 us
    pallas_call x1, Pallas kernels, per_device(): pl.pallas_call(start_kernel, out_shape=jax.ShapeDtypeStruct((boxes, local...  0.85 us
  transfers between devices with their start and end apart: 3, of which 0 were waited for; matrix products, arithmetic and copies ran while one was open for 0% of the time, Pallas kernels for 15%

profile of v10, /device:TPU:1, one launch (start us, length us, event | category | flops | bytes accessed | tf_op | source)
XLA Modules:
  0.0 33.7 jit_solution(10813195130780936714)
XLA Ops:
  0.6 0.9 %start.1.rows_ref = f32[2,16,512]{2,1,0:T(8,128)S(1)} custom-call(f32[2,4,16,512]{3,2,1,0:T(8,128)} %map_ref.5), custom_call_target="tpu_custom_call" | custom-call | tf_op jit(solution)/shard_map/start/pallas_call | solution.py:329
  1.5 2.1 %collective-permute-start = (f32[2,16,512]{2,1,0:T(8,128)S(1)}, f32[2,16,512]{2,1,0:T(8,128)S(1)}, u32[]{:S(2)}, u32[]{:S(2)}) collective-permute-start(f32[2,16,512]{2,1,0:T(8,128)S(1)} %start.1.rows_ref), channel_id=1, source_target_pairs={{0,8},{8,0},{16,24},{24,16},{32,40},{40,32},{48,56},{56,48},{64,72... | collective-permute-start | bytes 196616 | tf_op jit(solution)/shard_map/ppermute | solution.py:22
  3.6 2.8 %early.1 = (bf16[384,768]{1,0:T(8,128)(2,1)S(1)}, bf16[2048,512]{1,0:T(8,128)(2,1)S(1)}, f32[2048,768]{1,0:T(8,128)S(1)}, f32[2,3,16,512]{3,2,1,0:T(8,128)S(1)},...) custom-call(s32[1]{0:T(128)} %bitcast.place_ref, f32[2,16,512]{2,1,0:T(8,128)S(1)} %start.1.rows_ref, ...), custom_call_target="tpu_custom_call" | custom-call | flops 805306368 | bytes 6291456 | tf_op jit(solution)/shard_map/early/pallas_call | solution.py:346
  6.4 0.1 collective-permute-start.1
  6.6 0.0 collective-permute-done
  6.6 20.9 %all-gather = f32[16,16,896]{2,1,0:T(8,128)S(1)} all-gather(f32[2,16,896]{2,1,0:T(8,128)S(1)} %pad_maximum_fusion), channel_id=2, replica_groups=mesh['box'=32,'row'=8] {'row'}, dimensions={0}, use_global_device_ids=true | all-gather | bytes 1032192 | tf_op jit(solution)/shard_map/all_gather | solution.py:368
  27.5 0.0 collective-permute-done.1.other_ref
  27.5 1.6 %solve.1.solved_ref = bf16[128,1152]{1,0:T(8,128)(2,1)S(1)} custom-call(s32[1]{0:T(128)} %bitcast.place_ref, f32[8,2,16,896]{3,2,1,0:T(8,128)S(1)} %bitcast.3, bf16[384,768]{1,0:T(8,128)(2,1)S(1)} %get-tuple-element.22.own_ref.first_ref, bf16[384,768]{1,0:T(8,128)(2,1)S(1)} %collective-permute-done.1.other_ref), custom_call_target="tpu_custom_call" | custom-call | tf_op jit(solution)/shard_map/solve/pallas_call | solution.py:369
  29.2 0.2 collective-permute-start.2
  29.5 2.1 %middle.1 = (f32[2048,768]{1,0:T(8,128)S(1)}, bf16[2,2048,768]{2,1,0:T(8,128)(2,1)}, f32[2,3,16,768]{3,2,1,0:T(8,128)}) custom-call(s32[1]{0:T(128)} %bitcast.place_ref, f32[8,2,16,896]{3,2,1,0:T(8,128)S(1)} %bitcast.4, f32[2,3,16,512]{3,2,1,0:T(8,128)S(1)} %get-tuple-element.28.outer_ref, bf16[128,1152]{1,0:T(8,128)(2,1)S(1)} %solve.1.solved_ref, ...), custom_call_target="tpu_custom_call" | custom-call | flops 1610612736 | bytes 6291456 | tf_op jit(solution)/shard_map/middle/pallas_call | solution.py:408
  31.6 0.0 collective-permute-done.2.swapped_ref
  31.7 2.1 %field.1 = (bf16[2,2048,768]{2,1,0:T(8,128)(2,1)}, f32[2,3,16,768]{3,2,1,0:T(8,128)}) custom-call(s32[1]{0:T(128)} %bitcast.place_ref, f32[8,2,16,896]{3,2,1,0:T(8,128)S(1)} %bitcast.5, f32[2,3,16,512]{3,2,1,0:T(8,128)S(1)} %get-tuple-element.28.outer_ref, ...), custom_call_target="tpu_custom_call", output_to_operand_aliasing={{0}: (7, {}), {1}: (8, {})} | custom-call | tf_op jit(solution)/shard_map/field/pallas_call | solution.py:420
  (5 shorter events, 0.1 us)
Async XLA Ops:
  1.5 5.1 %collective-permute-start = (f32[2,16,512]{2,1,0:T(8,128)S(1)}, f32[2,16,512]{2,1,0:T(8,128)S(1)}, u32[]{:S(2)}, u32[]{:S(2)}) collective-permute-start(f32[2,16,512]{2,1,0:T(8,128)S(1)} %start.1.rows_ref), channel_id=1, source_target_pairs={{0,8},{8,0},{16,24},{24,16},{32,40},{40,32},{48,56},{56,48},{64,72... | collective-permute-start | bytes 196616 | tf_op jit(solution)/shard_map/ppermute | solution.py:22
  6.4 21.1 %collective-permute-start.1 = (bf16[384,768]{1,0:T(8,128)(2,1)S(1)}, bf16[384,768]{1,0:T(8,128)(2,1)S(1)}, u32[]{:S(2)}, u32[]{:S(2)}) collective-permute-start(bf16[384,768]{1,0:T(8,128)(2,1)S(1)} %get-tuple-element.22.own_ref.first_ref), channel_id=1, source_target_pairs={{0,8},{8,0},{16,24},{24,16},{32,40},{40,32},{48,56},{56,48},{64,72... | collective-permute-start | bytes 1769480 | tf_op jit(solution)/shard_map/ppermute | solution.py:22
  29.2 2.4 %collective-permute-start.2 = (bf16[128,1152]{1,0:T(8,128)(2,1)S(1)}, bf16[128,1152]{1,0:T(8,128)(2,1)S(1)}, u32[]{:S(2)}, u32[]{:S(2)}) collective-permute-start(bf16[128,1152]{1,0:T(8,128)(2,1)S(1)} %solve.1.solved_ref), channel_id=1, source_target_pairs={{0,1},{1,0},{2,3},{3,2},{4,5},{5,4},{6,7},{7,6},{8,9},{9,8},{10,11... | collective-permute-start | bytes 884744 | tf_op jit(solution)/shard_map/ppermute | solution.py:22

commit v11 on v10

--- a/solution.py
+++ b/solution.py
@@ -111,8 +111,11 @@
 
     @pl.when(level == 1)
     def _():
-        start_copies((data_copy, near_copy))
-        finish_copies((data_copy, near_copy))
+        copies = far_copies(
+            mine, map_ref, data_ref, operator_ref, outer_ref, second_ref, far_ref, arrived
+        )
+        start_copies((data_copy, near_copy) + copies[1:])
+        finish_copies((data_copy, near_copy) + copies[1:])
 
 
 def late_kernel(place_ref, solved_ref, map_ref, data_ref, operator_ref, first_ref, *refs):
@@ -125,9 +128,9 @@
 
     @pl.when(level == 1)
     def _():
-        start_copies(copies)
+        copies[0].start()
         first_product(first_ref, near_ref, partial_ref)
-        finish_copies(copies)
+        copies[0].wait()
 
 
 def solve_kernel(

time: 33.9 us -> 34.1 us (level)
  no operation moved by 1% of the time
where the time goes in v11:
time: 34.1 us; the launch traced here: 33.9 us
  blocking collectives  21.1 us (62%)
  Pallas kernels  9.59 us (28%)
  starting transfers between devices  2.5 us (7%)
  between operations  0.7 us (2%)
    all_gather x1, blocking collectives, per_device(): gathered = lax.all_gather(packed, 'row', axis=0)  21.1 us
    pallas_call x1, Pallas kernels, per_device(): pl.pallas_call(early_kernel, out_shape=(half,) + brought, in_specs=[SMEM_...  2.82 us
    ppermute x3, starting transfers between devices, exchange(): return lax.ppermute(value, axis, pairs)  2.5 us
    pallas_call x1, Pallas kernels, per_device(): pl.pallas_call(middle_kernel, out_shape=(part,) + outputs, in_specs=[SMEM...  2.15 us
    pallas_call x1, Pallas kernels, per_device(): pl.pallas_call(field_kernel, out_shape=outputs, in_specs=[SMEM_SPEC] + [V...  2.08 us
    pallas_call x1, Pallas kernels, per_device(): pl.pallas_call(solve_kernel, out_shape=jax.ShapeDtypeStruct((edge, loads...  1.65 us
    pallas_call x1, Pallas kernels, per_device(): pl.pallas_call(start_kernel, out_shape=jax.ShapeDtypeStruct((boxes, local...  0.85 us
  transfers between devices with their start and end apart: 3, of which 0 were waited for; matrix products, arithmetic and copies ran while one was open for 0% of the time, Pallas kernels for 15%

profile of v11, /device:TPU:1, one launch (start us, length us, event | category | flops | bytes accessed | tf_op | source)
XLA Modules:
  0.0 33.9 jit_solution(320776908734094068)
XLA Ops:
  0.6 0.9 %start.1.rows_ref = f32[2,16,512]{2,1,0:T(8,128)S(1)} custom-call(f32[2,4,16,512]{3,2,1,0:T(8,128)} %map_ref.5), custom_call_target="tpu_custom_call" | custom-call | tf_op jit(solution)/shard_map/start/pallas_call | solution.py:332
  1.5 2.1 %collective-permute-start = (f32[2,16,512]{2,1,0:T(8,128)S(1)}, f32[2,16,512]{2,1,0:T(8,128)S(1)}, u32[]{:S(2)}, u32[]{:S(2)}) collective-permute-start(f32[2,16,512]{2,1,0:T(8,128)S(1)} %start.1.rows_ref), channel_id=1, source_target_pairs={{0,8},{8,0},{16,24},{24,16},{32,40},{40,32},{48,56},{56,48},{64,72... | collective-permute-start | bytes 196616 | tf_op jit(solution)/shard_map/ppermute | solution.py:22
  3.6 2.8 %early.1 = (bf16[384,768]{1,0:T(8,128)(2,1)S(1)}, bf16[2048,512]{1,0:T(8,128)(2,1)S(1)}, f32[2048,768]{1,0:T(8,128)S(1)}, f32[2,3,16,512]{3,2,1,0:T(8,128)S(1)},...) custom-call(s32[1]{0:T(128)} %bitcast.place_ref, f32[2,16,512]{2,1,0:T(8,128)S(1)} %start.1.rows_ref, ...), custom_call_target="tpu_custom_call" | custom-call | flops 805306368 | bytes 6291456 | tf_op jit(solution)/shard_map/early/pallas_call | solution.py:349
  6.4 0.1 collective-permute-start.1
  6.6 0.0 collective-permute-done
  6.6 21.1 %all-gather = f32[16,16,896]{2,1,0:T(8,128)S(1)} all-gather(f32[2,16,896]{2,1,0:T(8,128)S(1)} %pad_maximum_fusion), channel_id=2, replica_groups=mesh['box'=32,'row'=8] {'row'}, dimensions={0}, use_global_device_ids=true | all-gather | bytes 1032192 | tf_op jit(solution)/shard_map/all_gather | solution.py:371
  27.7 0.0 collective-permute-done.1.other_ref
  27.7 1.6 %solve.1.solved_ref = bf16[128,1152]{1,0:T(8,128)(2,1)S(1)} custom-call(s32[1]{0:T(128)} %bitcast.place_ref, f32[8,2,16,896]{3,2,1,0:T(8,128)S(1)} %bitcast.3, bf16[384,768]{1,0:T(8,128)(2,1)S(1)} %get-tuple-element.22.own_ref.first_ref, bf16[384,768]{1,0:T(8,128)(2,1)S(1)} %collective-permute-done.1.other_ref), custom_call_target="tpu_custom_call" | custom-call | tf_op jit(solution)/shard_map/solve/pallas_call | solution.py:372
  29.4 0.2 collective-permute-start.2
  29.7 2.1 %middle.1 = (f32[2048,768]{1,0:T(8,128)S(1)}, bf16[2,2048,768]{2,1,0:T(8,128)(2,1)}, f32[2,3,16,768]{3,2,1,0:T(8,128)}) custom-call(s32[1]{0:T(128)} %bitcast.place_ref, f32[8,2,16,896]{3,2,1,0:T(8,128)S(1)} %bitcast.4, f32[2,3,16,512]{3,2,1,0:T(8,128)S(1)} %get-tuple-element.28.outer_ref, bf16[128,1152]{1,0:T(8,128)(2,1)S(1)} %solve.1.solved_ref, ...), custom_call_target="tpu_custom_call" | custom-call | flops 1610612736 | bytes 6291456 | tf_op jit(solution)/shard_map/middle/pallas_call | solution.py:411
  31.8 0.0 collective-permute-done.2.swapped_ref
  31.8 2.1 %field.1 = (bf16[2,2048,768]{2,1,0:T(8,128)(2,1)}, f32[2,3,16,768]{3,2,1,0:T(8,128)}) custom-call(s32[1]{0:T(128)} %bitcast.place_ref, f32[8,2,16,896]{3,2,1,0:T(8,128)S(1)} %bitcast.5, f32[2,3,16,512]{3,2,1,0:T(8,128)S(1)} %get-tuple-element.28.outer_ref, ...), custom_call_target="tpu_custom_call", output_to_operand_aliasing={{0}: (7, {}), {1}: (8, {})} | custom-call | tf_op jit(solution)/shard_map/field/pallas_call | solution.py:423
  (5 shorter events, 0.1 us)
Async XLA Ops:
  1.5 5.1 %collective-permute-start = (f32[2,16,512]{2,1,0:T(8,128)S(1)}, f32[2,16,512]{2,1,0:T(8,128)S(1)}, u32[]{:S(2)}, u32[]{:S(2)}) collective-permute-start(f32[2,16,512]{2,1,0:T(8,128)S(1)} %start.1.rows_ref), channel_id=1, source_target_pairs={{0,8},{8,0},{16,24},{24,16},{32,40},{40,32},{48,56},{56,48},{64,72... | collective-permute-start | bytes 196616 | tf_op jit(solution)/shard_map/ppermute | solution.py:22
  6.4 21.3 %collective-permute-start.1 = (bf16[384,768]{1,0:T(8,128)(2,1)S(1)}, bf16[384,768]{1,0:T(8,128)(2,1)S(1)}, u32[]{:S(2)}, u32[]{:S(2)}) collective-permute-start(bf16[384,768]{1,0:T(8,128)(2,1)S(1)} %get-tuple-element.22.own_ref.first_ref), channel_id=1, source_target_pairs={{0,8},{8,0},{16,24},{24,16},{32,40},{40,32},{48,56},{56,48},{64,72... | collective-permute-start | bytes 1769480 | tf_op jit(solution)/shard_map/ppermute | solution.py:22
  29.4 2.4 %collective-permute-start.2 = (bf16[128,1152]{1,0:T(8,128)(2,1)S(1)}, bf16[128,1152]{1,0:T(8,128)(2,1)S(1)}, u32[]{:S(2)}, u32[]{:S(2)}) collective-permute-start(bf16[128,1152]{1,0:T(8,128)(2,1)S(1)} %solve.1.solved_ref), channel_id=1, source_target_pairs={{0,1},{1,0},{2,3},{3,2},{4,5},{5,4},{6,7},{7,6},{8,9},{9,8},{10,11... | collective-permute-start | bytes 884744 | tf_op jit(solution)/shard_map/ppermute | solution.py:22
